TPU v7x, 128 devices: a whole 4x4x4 slice. The times are simulated.
128 devices in a mesh: gx: 8 (over y, core), gy: 16 (over x, z).
Axes of the slice: x: 4, y: 4, z: 4, core: 2. Of those that a mesh axis runs over, the one named last changes fastest.
Arguments:
- log_perm: float32 [64, 512, 128], P('gx', 'gy'), may hold values from -4 to 4
- perturb: float32 [64, 512, 128], P('gx', 'gy'), may hold values from -6 to 6
- storage: float32 [64, 512, 128], P('gx', 'gy'), may hold values from 0.03 to 1
- base_press: float32 [2, 64, 512, 128], P(None, 'gx', 'gy'), may hold values from -6 to 6
- well_rows: float32 [16384, 512], P(('gx', 'gy')), may hold values from 0.002 to 0.02
- well_cells: int32 [16384], P(('gx', 'gy')), may hold values from 0 to 32767
- well_counts: int32 [16384], P(('gx', 'gy')), may hold values from 1 to 512, as said below
- well_owner: int32 [16384, 1], P(('gx', 'gy')), may hold values from 0 to 127; in each aligned block of 128 rows (0 to 127, 128 to 255, ...) at most 2 rows name the same one
- well_start: int32 [16384], P(('gx', 'gy')), may hold values from 0 to 1
Outputs:
- hess_action: float32 [64, 512, 128], P('gx', 'gy')
- final_change: float32 [64, 512, 128], P('gx', 'gy')
Inputs may be any that keep to these rules, and one draw needn't show every extreme that they name: `well_owner`: names the device, counted as gx index times 16 plus gy index, whose tile holds the well; among the wells listed on one device no owner appears more than 2 times, and in every draw some device names some owner exactly 2 times. `well_cells`: index x * 32 * 128 + y * 128 + z of the well's cell within its owner's tile. `well_counts`: every draw has a well with all 512 samples and one with a single sample.
All inputs are finite; a program needn't handle non-finite values.
Results may differ from a plain program's by a relative error of at most 0.0001.
Values sent between devices are 32-bit elements; how exact they have to be, the bound alone decides.
A program may use at most 128 MiB of HBM per device.

v0:
```python
import jax
import jax.numpy as jnp
from jax import lax
from jax.sharding import PartitionSpec as P

TSTEPS = 2
VCYCLES = 2
SWEEPS = 2
CSWEEPS = 4
SAMPLES = 512
CAP = 2


OMEGA = 0.8


def extended(block, sides, width):
    for axis, dim in sides:
        count = lax.axis_size(axis)
        forward = [(i, i + 1) for i in range(count - 1)]
        backward = [(target, source) for source, target in forward]
        low = lax.ppermute(
            lax.slice_in_dim(block, block.shape[dim] - width, None, axis=dim), axis, forward
        )
        high = lax.ppermute(lax.slice_in_dim(block, 0, width, axis=dim), axis, backward)
        block = jnp.concatenate([low, block, high], axis=dim)
    return block


def lower_pad(values):
    return jnp.pad(values, ((0, 0), (0, 0), (0, 1)))


def upper_pad(values):
    return jnp.pad(values, ((0, 0), (0, 0), (1, 0)))


def fine_rim(values):
    return extended(values, (("gx", 1), ("gy", 2)), 1)


def middle_rim(values):
    return extended(values, (("gx", 1), ("gy", 2)), 1)


def coarse_rim(values):
    return extended(values, (("gx", 1), ("gy", 2)), 1)


def coarsen(values):
    size_x, size_y, size_z = values.shape
    return values.reshape(size_x // 2, 2, size_y // 2, 2, size_z // 2, 2).mean(axis=(1, 3, 5))


def prolong(values):
    return jnp.repeat(jnp.repeat(jnp.repeat(values, 2, 0), 2, 1), 2, 2)


def coefficients(log_pad, storage_level, factor):
    center = log_pad[1:-1, 1:-1]
    along_x = factor * jnp.exp(0.5 * (log_pad[:-1, 1:-1] + log_pad[1:, 1:-1]))
    along_y = factor * jnp.exp(0.5 * (log_pad[1:-1, :-1] + log_pad[1:-1, 1:]))
    along_z = factor * jnp.exp(0.5 * (center[:, :, :-1] + center[:, :, 1:]))
    diagonal = storage_level + along_x[1:] + along_x[:-1] + along_y[:, 1:] + along_y[:, :-1]
    diagonal = diagonal + lower_pad(along_z) + upper_pad(along_z)
    return (along_x, along_y, along_z, diagonal)


def apply_operator(value_pad, coeffs):
    along_x, along_y, along_z, diagonal = coeffs
    center = value_pad[1:-1, 1:-1]
    beside = along_x[1:] * value_pad[2:, 1:-1] + along_x[:-1] * value_pad[:-2, 1:-1]
    beside = beside + along_y[:, 1:] * value_pad[1:-1, 2:] + along_y[:, :-1] * value_pad[1:-1, :-2]
    beside = beside + lower_pad(along_z * center[:, :, 1:]) + upper_pad(along_z * center[:, :, :-1])
    return diagonal * center - beside


def perturbed(pressure_pad, change_pad, coeffs):
    along_x, along_y, along_z, diagonal = coeffs
    pressure = pressure_pad[1:-1, 1:-1]
    change = change_pad[1:-1, 1:-1]
    summed = (
        along_x[1:] * 0.5 * (change + change_pad[2:, 1:-1]) * (pressure - pressure_pad[2:, 1:-1])
    )
    summed = summed + along_x[:-1] * 0.5 * (change + change_pad[:-2, 1:-1]) * (
        pressure - pressure_pad[:-2, 1:-1]
    )
    summed = summed + along_y[:, 1:] * 0.5 * (change + change_pad[1:-1, 2:]) * (
        pressure - pressure_pad[1:-1, 2:]
    )
    summed = summed + along_y[:, :-1] * 0.5 * (change + change_pad[1:-1, :-2]) * (
        pressure - pressure_pad[1:-1, :-2]
    )
    vertical = (
        along_z
        * 0.5
        * (change[:, :, :-1] + change[:, :, 1:])
        * (pressure[:, :, :-1] - pressure[:, :, 1:])
    )
    return summed + lower_pad(vertical) - upper_pad(vertical)


def curvature(pressure_pad, adjoint_pad, coeffs):
    along_x, along_y, along_z, diagonal = coeffs
    pressure = pressure_pad[1:-1, 1:-1]
    adjoint = adjoint_pad[1:-1, 1:-1]
    summed = (
        0.5 * along_x[1:] * (pressure - pressure_pad[2:, 1:-1]) * (adjoint - adjoint_pad[2:, 1:-1])
    )
    summed = summed + 0.5 * along_x[:-1] * (pressure - pressure_pad[:-2, 1:-1]) * (
        adjoint - adjoint_pad[:-2, 1:-1]
    )
    summed = summed + 0.5 * along_y[:, 1:] * (pressure - pressure_pad[1:-1, 2:]) * (
        adjoint - adjoint_pad[1:-1, 2:]
    )
    summed = summed + 0.5 * along_y[:, :-1] * (pressure - pressure_pad[1:-1, :-2]) * (
        adjoint - adjoint_pad[1:-1, :-2]
    )
    vertical = (
        0.5
        * along_z
        * (pressure[:, :, :-1] - pressure[:, :, 1:])
        * (adjoint[:, :, :-1] - adjoint[:, :, 1:])
    )
    return summed + lower_pad(vertical) + upper_pad(vertical)


def jacobi_sweep(iterate, right_side, coeffs, padder):
    if iterate is None:
        return OMEGA * right_side / coeffs[3]
    padded = padder(iterate[None])[0]
    return iterate + OMEGA * (right_side - apply_operator(padded, coeffs)) / coeffs[3]


def vcycle(iterate, right_side, fine_coeffs, middle_coeffs, fine_pad, middle_pad, coarse_solve):
    current = iterate
    for sweep_index in range(SWEEPS):
        current = jacobi_sweep(current, right_side, fine_coeffs, fine_pad)
    residual = right_side - apply_operator(fine_pad(current[None])[0], fine_coeffs)
    middle_side = coarsen(residual)
    middle = None
    for sweep_index in range(SWEEPS):
        middle = jacobi_sweep(middle, middle_side, middle_coeffs, middle_pad)
    middle_res = middle_side - apply_operator(middle_pad(middle[None])[0], middle_coeffs)
    middle = middle + prolong(coarse_solve(coarsen(middle_res)))
    for sweep_index in range(SWEEPS):
        middle = jacobi_sweep(middle, middle_side, middle_coeffs, middle_pad)
    current = current + prolong(middle)
    for sweep_index in range(SWEEPS):
        current = jacobi_sweep(current, right_side, fine_coeffs, fine_pad)
    return current


def multigrid_solve(right_side, fine_coeffs, middle_coeffs, fine_pad, middle_pad, coarse_solve):
    current = None
    for cycle_index in range(VCYCLES):
        current = vcycle(
            current, right_side, fine_coeffs, middle_coeffs, fine_pad, middle_pad, coarse_solve
        )
    return current


def well_weights(records, counts, starts):
    sample_pos = jnp.arange(SAMPLES, dtype=jnp.int32)
    counted = jnp.where(sample_pos[None, :] < counts[:, None], records, 0.0)
    per_step = counted.reshape(records.shape[0], TSTEPS, SAMPLES // TSTEPS).sum(axis=2)
    step_pos = jnp.arange(TSTEPS, dtype=jnp.int32)
    return jnp.where(step_pos[None, :] >= starts[:, None], per_step, 0.0)


def local(
    log_perm,
    perturb,
    storage,
    base_press,
    well_rows,
    well_cells,
    well_counts,
    well_owner,
    well_start,
):
    devices = lax.axis_size("gx") * lax.axis_size("gy")
    owner_ids = well_owner[:, 0]
    listed = owner_ids.shape[0]
    same_owner = owner_ids[:, None] == owner_ids[None, :]
    earlier = (
        jnp.arange(listed, dtype=jnp.int32)[None, :] < jnp.arange(listed, dtype=jnp.int32)[:, None]
    )
    slot_rank = jnp.sum(jnp.logical_and(same_owner, earlier), axis=1)
    slot_index = owner_ids * CAP + slot_rank
    slot_total = devices * CAP
    send_rows = jnp.zeros((slot_total, SAMPLES), jnp.float32).at[slot_index].set(well_rows)
    packed = jnp.stack([well_cells, well_counts, well_start], axis=1)
    send_ints = jnp.zeros((slot_total, 3), jnp.int32).at[slot_index].set(packed)
    got_rows, got_ints = (
        lax.all_to_all(send_rows, ("gx", "gy"), split_axis=0, concat_axis=0, tiled=True),
        lax.all_to_all(send_ints, ("gx", "gy"), split_axis=0, concat_axis=0, tiled=True),
    )
    weights = well_weights(got_rows, got_ints[:, 1], got_ints[:, 2])
    cell_ids = got_ints[:, 0]
    source = jnp.zeros((TSTEPS, log_perm.size), jnp.float32).at[:, cell_ids].add(weights.T)
    source = source.reshape((TSTEPS,) + log_perm.shape)
    padded = fine_rim(jnp.concatenate([log_perm[None], perturb[None], base_press], axis=0))
    fine_coeffs = coefficients(padded[0], storage, 1.0)
    middle_log = coarsen(log_perm)
    middle_store = coarsen(storage)
    middle_coeffs = coefficients(middle_rim(middle_log[None])[0], middle_store, 0.25)
    coarse_log = coarsen(middle_log)
    coarse_store = coarsen(middle_store)
    coarse_coeffs = coefficients(coarse_rim(coarse_log[None])[0], coarse_store, 0.0625)

    def coarse_solve(right_side):
        iterate = None
        for sweep_index in range(CSWEEPS):
            iterate = jacobi_sweep(iterate, right_side, coarse_coeffs, coarse_rim)
        return iterate

    def solve_field(right_side):
        return multigrid_solve(
            right_side, fine_coeffs, middle_coeffs, fine_rim, middle_rim, coarse_solve
        )

    previous = jnp.zeros(log_perm.shape, jnp.float32)
    changes = []
    for step_index in range(TSTEPS):
        right_side = storage * previous - perturbed(padded[2 + step_index], padded[1], fine_coeffs)
        previous = solve_field(right_side)
        changes.append(previous)
    adjoint_next = jnp.zeros(log_perm.shape, jnp.float32)
    adjoints = [None] * TSTEPS
    for step_index in range(TSTEPS - 1, -1, -1):
        right_side = storage * adjoint_next + source[step_index] * changes[step_index]
        adjoint_next = solve_field(right_side)
        adjoints[step_index] = adjoint_next
    adjoint_pad = fine_rim(jnp.stack(adjoints))
    hessian = jnp.zeros(log_perm.shape, jnp.float32)
    for step_index in range(TSTEPS):
        hessian = hessian - curvature(padded[2 + step_index], adjoint_pad[step_index], fine_coeffs)
    return (hessian, changes[-1])


def solution(mesh):
    return jax.shard_map(
        local,
        mesh=mesh,
        in_specs=(
            P("gx", "gy", None),
            P("gx", "gy", None),
            P("gx", "gy", None),
            P(None, "gx", "gy", None),
            P(("gx", "gy"), None),
            P(("gx", "gy")),
            P(("gx", "gy")),
            P(("gx", "gy"), None),
            P(("gx", "gy")),
        ),
        out_specs=(P("gx", "gy", None), P("gx", "gy", None)),
        check_vma=False,
    )
```

profile of v0, /device:TPU:3, one launch (start us, length us, event | category | flops | bytes accessed | tf_op | source)
XLA Modules:
  0.0 1807.4 jit_solution(4703470336424815088)
XLA Ops:
  7.3 10.5 reshape.257
  30.7 9.7 reshape.256
  48.2 5.6 collective-permute-start.27
  55.9 5.5 collective-permute-start.3
  63.3 5.5 collective-permute-start.15
  77.9 5.5 collective-permute-start.7
  107.2 9.7 reshape.255
  323.9 9.7 reshape.265
  339.6 5.4 collective-permute-start.68
  524.1 9.7 reshape.273
  708.9 5.4 collective-permute-start.152
  740.6 9.7 reshape.281
  864.8 6.7 all-to-all-start
  890.5 7.0 all-to-all-start.1
  917.8 8.5 scatter_custom_fusion.2
  932.4 20.6 %slice_reduce_fusion = (f32[32768]{0:T(1024)S(1)}, f32[32768]{0:T(1024)S(1)}) fusion(f32[2,32768]{0,1:T(8,128)} %scatter_custom_fusion.2), kind=kLoop, calls=%fused_computation.3 | loop fusion | bytes 524288 | tf_op jit(solution)/shard_map/slice | solution.py:232
  960.3 5.5 collective-permute-start.199
  974.7 5.5 collective-permute-start.200
  989.7 9.7 reshape.289
  1206.2 9.7 reshape.297
  1221.9 5.4 collective-permute-start.252
  1357.4 5.4 collective-permute-start.284
  1406.1 9.7 reshape.305
  1622.9 9.7 reshape.313
  (1495 shorter events, 1603.4 us)
Async XLA Ops:
  1.5 54.3 %collective-permute-start.1 = (f32[4,1,32,128]{3,2,1,0:T(8,128)S(1)}, f32[4,1,32,128]{3,2,1,0:T(8,128)S(1)}, u32[]{:S(2)}, u32[]{:S(2)}) collective-permute-start(f32[4,1,32,128]{3,2,1,0:T(8,128)S(1)} %get-tuple-element.28), channel_id=1, source_target_pairs={{16,0},{32,16},{48,32},{64,48},{80,64},{96,80},{112,96},{17,1},{33... | collective-permute-start | bytes 196616 | tf_op jit(solution)/shard_map/ppermute | solution.py:25
  4.1 51.7 %collective-permute-start = (f32[4,1,32,128]{3,2,1,0:T(8,128)S(1)}, f32[4,1,32,128]{3,2,1,0:T(8,128)S(1)}, u32[]{:S(2)}, u32[]{:S(2)}) collective-permute-start(f32[4,1,32,128]{3,2,1,0:T(8,128)S(1)} %get-tuple-element.27), channel_id=1, source_target_pairs={{0,16},{16,32},{32,48},{48,64},{64,80},{80,96},{96,112},{1,17},{17... | collective-permute-start | bytes 196616 | tf_op jit(solution)/shard_map/ppermute | solution.py:22
  23.0 21.4 %collective-permute-start.25 = (f32[1,1,8,32]{3,2,1,0:T(8,128)S(1)}, f32[1,1,8,32]{3,2,1,0:T(8,128)S(1)}, u32[]{:S(2)}, u32[]{:S(2)}) collective-permute-start(f32[1,1,8,32]{3,2,1,0:T(8,128)S(1)} %get-tuple-element.603), channel_id=1, source_target_pairs={{16,0},{32,16},{48,32},{64,48},{80,64},{96,80},{112,96},{17,1},{33... | collective-permute-start | bytes 3080 | tf_op jit(solution)/shard_map/ppermute | solution.py:25
  25.0 23.2 %collective-permute-start.24 = (f32[1,1,8,32]{3,2,1,0:T(8,128)S(1)}, f32[1,1,8,32]{3,2,1,0:T(8,128)S(1)}, u32[]{:S(2)}, u32[]{:S(2)}) collective-permute-start(f32[1,1,8,32]{3,2,1,0:T(8,128)S(1)} %get-tuple-element.602), channel_id=1, source_target_pairs={{0,16},{16,32},{32,48},{48,64},{64,80},{80,96},{96,112},{1,17},{17... | collective-permute-start | bytes 3080 | tf_op jit(solution)/shard_map/ppermute | solution.py:22
  28.7 25.1 %collective-permute-start.13 = (f32[1,1,16,64]{3,2,1,0:T(8,128)S(1)}, f32[1,1,16,64]{3,2,1,0:T(8,128)S(1)}, u32[]{:S(2)}, u32[]{:S(2)}) collective-permute-start(f32[1,1,16,64]{3,2,1,0:T(8,128)S(1)} %get-tuple-element.503), channel_id=1, source_target_pairs={{16,0},{32,16},{48,32},{64,48},{80,64},{96,80},{112,96},{17,1},{33... | collective-permute-start | bytes 12296 | tf_op jit(solution)/shard_map/ppermute | solution.py:25
  44.5 11.3 collective-permute-start.12
  48.2 80.2 %collective-permute-start.27 = (f32[1,4,1,32]{3,2,1,0:T(1,128)S(1)}, f32[1,4,1,32]{3,2,1,0:T(1,128)S(1)}, u32[]{:S(2)}, u32[]{:S(2)}) collective-permute-start(f32[1,4,1,32]{3,2,1,0:T(1,128)S(1)} %get-tuple-element.553), channel_id=1, source_target_pairs={{1,0},{2,1},{3,2},{4,3},{5,4},{6,5},{7,6},{8,7},{9,8},{10,9},{11,1... | collective-permute-start | bytes 1544 | tf_op jit(solution)/shard_map/ppermute | solution.py:25
  53.8 74.6 %collective-permute-start.26 = (f32[1,4,1,32]{3,2,1,0:T(1,128)S(1)}, f32[1,4,1,32]{3,2,1,0:T(1,128)S(1)}, u32[]{:S(2)}, u32[]{:S(2)}) collective-permute-start(f32[1,4,1,32]{3,2,1,0:T(1,128)S(1)} %get-tuple-element.552), channel_id=1, source_target_pairs={{0,1},{1,2},{2,3},{3,4},{4,5},{5,6},{6,7},{7,8},{8,9},{9,10},{10,1... | collective-permute-start | bytes 1544 | tf_op jit(solution)/shard_map/ppermute | solution.py:22
  55.9 12.9 collective-permute-start.3
  61.3 9.4 collective-permute-start.2
  63.3 10.2 collective-permute-start.15
  68.8 8.3 collective-permute-start.14
  855.8 15.6 collective-permute-start.185
  857.8 13.7 collective-permute-start.184
  864.8 25.8 %all-to-all-start = ((s32[128,2,3]{2,1,0:T(2,128)}), s32[128,2,3]{2,1,0:T(2,128)S(1)}, u32[]{:S(2)}, u32[]{:S(2)}) async-start(s32[128,2,3]{2,1,0:T(2,128)} %bitcast.10), calls=%async_computation | async-start | bytes 262144 | tf_op jit(solution)/shard_map/all_to_all | solution.py:197
  871.5 9.6 collective-permute-start.187
  883.8 14.0 collective-permute-start.189
  887.5 10.3 collective-permute-start.188
  890.5 19.2 %all-to-all-start.1 = ((f32[128,2,512]{2,1,0:T(2,128)}), f32[128,2,512]{2,1,0:T(2,128)S(1)}, u32[]{:S(2)}, u32[]{:S(2)}) async-start(f32[128,2,512]{2,1,0:T(2,128)} %all_to_all.19), calls=%async_computation.1 | async-start | bytes 1048576 | tf_op jit(solution)/shard_map/all_to_all | solution.py:196
  897.8 12.6 collective-permute-start.191
  910.7 15.5 collective-permute-start.193
  914.0 12.3 collective-permute-start.192
  926.3 26.7 %collective-permute-start.195 = (f32[1,10,1,128]{3,2,1,0:T(1,128)S(1)}, f32[1,10,1,128]{3,2,1,0:T(1,128)S(1)}, u32[]{:S(2)}, u32[]{:S(2)}) collective-permute-start(f32[1,10,1,128]{3,2,1,0:T(1,128)S(1)} %get-tuple-element.144), channel_id=1, source_target_pairs={{1,0},{2,1},{3,2},{4,3},{5,4},{6,5},{7,6},{8,7},{9,8},{10,9},{11,1... | collective-permute-start | bytes 15368 | tf_op jit(solution)/shard_map/ppermute | solution.py:25
  930.2 22.7 %collective-permute-start.194 = (f32[1,10,1,128]{3,2,1,0:T(1,128)S(1)}, f32[1,10,1,128]{3,2,1,0:T(1,128)S(1)}, u32[]{:S(2)}, u32[]{:S(2)}) collective-permute-start(f32[1,10,1,128]{3,2,1,0:T(1,128)S(1)} %get-tuple-element.143), channel_id=1, source_target_pairs={{0,1},{1,2},{2,3},{3,4},{4,5},{5,6},{6,7},{7,8},{8,9},{9,10},{10,1... | collective-permute-start | bytes 15368 | tf_op jit(solution)/shard_map/ppermute | solution.py:22
  (370 other events, 2824.1 us)
where the time goes:
time: 1830 us; the launch traced here: 1810 us
  starting transfers between devices  1220 us (67%)
  waiting for transfers between devices  355 us (19%)
  local copies, waits for them, and re-layouts  141 us (8%)
  other arithmetic  79.1 us (4%)
    ppermute x192, starting transfers between devices, extended(): lax.ppermute(lax.slice_in_dim(block, block.shape[dim] - width, None, axis...  811 us
    ppermute x192, starting transfers between devices, extended(): lax.ppermute(lax.slice_in_dim(block, 0, width, axis=dim), axis, backward)  399 us
    ppermute x192, waiting for transfers between devices, extended(): lax.ppermute(lax.slice_in_dim(block, block.shape[dim] - width, None, axis...  349 us
    reshape x18, local copies, waits for them, and re-layouts, coarsen(): values.reshape(size_x // 2, 2, size_y // 2, 2, size_z // 2, 2)  107 us
    reduce_sum x20, other arithmetic, coarsen(): values.reshape(size_x // 2, 2, size_y // 2, 2, size_z // 2, 2)  41.7 us
  transfers between devices with their start and end apart: 386, of which 182 were waited for; matrix products, arithmetic and copies ran while one was open for 4% of the time, Pallas kernels for 0%

commit v1 on v0

v1 whole, which is shorter than its diff:
```python
import jax
import jax.numpy as jnp
from jax import lax
from jax.experimental import pallas as pl
from jax.experimental.pallas import tpu as pltpu
from jax.sharding import PartitionSpec as P

TSTEPS = 2
VCYCLES = 2
SAMPLES = 512
CAP = 2
OMEGA = 0.8

F32 = jnp.float32
MESH = pl.DeviceIdType.MESH

CX0, CY0, H0, W0 = 8, 32, 5, 5
CX1, CY1, H1, W1 = 4, 16, 3, 3
CX2, CY2, H2 = 2, 8, 4
HY = 8
NX0, NY0 = CX0 + 2 * H0, CY0 + 2 * HY
NX1, NY1 = CX1 + 2 * H1, CY1 + 2 * HY
NX2, NY2 = CX2 + 2 * H2, CY2 + 2 * HY
NZ = 128

NEAR = [(dx, dy) for dx in (-1, 0, 1) for dy in (-1, 0, 1) if (dx, dy) != (0, 0)]
FACES = [(-1, 0), (1, 0), (0, -1), (0, 1)]
WIDE = [(dx, dy) for dx in (-2, -1, 0, 1, 2) for dy in (-1, 0, 1) if (dx, dy) != (0, 0)]


def span_x(dx, core, halo, width):
    if dx > 0:
        return pl.ds(halo + core - width, width), pl.ds(halo - width, width)
    if dx < 0:
        return pl.ds(halo, width), pl.ds(halo + core, width)
    return pl.ds(halo, core), pl.ds(halo, core)


def span_y(dy, core):
    if dy > 0:
        return pl.ds(core, HY), pl.ds(0, HY)
    if dy < 0:
        return pl.ds(HY, HY), pl.ds(HY + core, HY)
    return pl.ds(HY, core), pl.ds(HY, core)


def span_tile(dx):
    return pl.ds(H2, CX2), pl.ds(H2 - CX2 * dx, CX2)


def swap_pair(values, stride):
    lane = lax.broadcasted_iota(jnp.int32, values.shape, values.ndim - 1)
    axis = values.ndim - 1
    return jnp.where(
        (lane & stride) == 0,
        pltpu.roll(values, NZ - stride, axis),
        pltpu.roll(values, stride, axis),
    )


def kernel(
    gx_count,
    gy_count,
    log_ref,
    pert_ref,
    stor_ref,
    press_ref,
    src_ref,
    hess_ref,
    final_ref,
    ms0,
    ms1,
    ms2,
    pp,
    xa,
    xb,
    bb,
    a0,
    dinv0,
    dg0,
    r0,
    b1,
    e1a,
    e1b,
    a1,
    dinv1,
    dg1,
    r1,
    b2,
    e2a,
    e2b,
    a2,
    dinv2,
    pair,
    prev,
    dps,
    s_ms0,
    s_ms1,
    s_ms2,
    s_pp,
    s_bb,
    s_x,
    s_b1,
    s_b2,
):
    gx = lax.axis_index("gx")
    gy = lax.axis_index("gy")

    def exists(dx, dy):
        tx, ty = gx + dx, gy + dy
        ok = None
        for cond in (
            [tx >= 0] * (dx < 0) + [tx < gx_count] * (dx > 0)
            + [ty >= 0] * (dy < 0) + [ty < gy_count] * (dy > 0)
        ):
            ok = cond if ok is None else jnp.logical_and(ok, cond)
        return ok

    def copies(offsets, sems, views):
        made = []
        for index, (dx, dy) in enumerate(offsets):
            source, target = views(dx, dy)
            made.append(
                (
                    dx,
                    dy,
                    pltpu.make_async_remote_copy(
                        src_ref=source,
                        dst_ref=target,
                        send_sem=sems.at[0, index],
                        recv_sem=sems.at[1, index],
                        device_id=(gx + dx, gy + dy),
                        device_id_type=MESH,
                    ),
                )
            )
        return made

    def start(made):
        for dx, dy, copy in made:
            pl.when(exists(dx, dy))(copy.start)

    def finish(made):
        for dx, dy, copy in made:
            pl.when(exists(-dx, -dy))(copy.wait_recv)
        for dx, dy, copy in made:
            pl.when(exists(dx, dy))(copy.wait_send)

    def views0(ref, width):
        def at(dx, dy):
            sx, tx = span_x(dx, CX0, H0, width)
            sy, ty = span_y(dy, CY0)
            return ref.at[sx, sy], ref.at[tx, ty]

        return at

    def views0s(ref, width):
        def at(dx, dy):
            sx, tx = span_x(dx, CX0, H0, width)
            sy, ty = span_y(dy, CY0)
            return ref.at[:, sx, sy], ref.at[:, tx, ty]

        return at

    def views1(ref):
        def at(dx, dy):
            sx, tx = span_x(dx, CX1, H1, W1)
            sy, ty = span_y(dy, CY1)
            return ref.at[sx, sy], ref.at[tx, ty]

        return at

    def views1s(ref):
        def at(dx, dy):
            sx, tx = span_x(dx, CX1, H1, W1)
            sy, ty = span_y(dy, CY1)
            return ref.at[:, sx, sy], ref.at[:, tx, ty]

        return at

    def views2(ref):
        def at(dx, dy):
            sx, tx = span_tile(dx)
            sy, ty = span_y(dy, CY2)
            return ref.at[sx, sy], ref.at[tx, ty]

        return at

    def views2s(ref):
        def at(dx, dy):
            sx, tx = span_tile(dx)
            sy, ty = span_y(dy, CY2)
            return ref.at[:, sx, sy], ref.at[:, tx, ty]

        return at

    def halve(first, second, size, stride):
        pair[pl.ds(0, 2 * size), :] = first + second
        summed = pair[pl.ds(0, size, stride=2), :] + pair[pl.ds(1, size, stride=2), :]
        return 0.125 * (summed + swap_pair(summed, stride))

    def double(values, size):
        pair[pl.ds(0, size, stride=2), :] = values
        pair[pl.ds(1, size, stride=2), :] = values
        return pair[pl.ds(0, 2 * size), :]

    y0, y1, y2 = pl.ds(HY, CY0), pl.ds(HY, CY1), pl.ds(HY, CY2)

    for ref in (ms0, ms1, ms2, pp, xa, xb, bb, b1, e1a, e1b, b2, e2a, e2b, a0, a1, a2):
        ref[...] = jnp.zeros(ref.shape, F32)
    prev[...] = jnp.zeros(prev.shape, F32)
    hess_ref[...] = jnp.zeros(hess_ref.shape, F32)
    for i in range(CX0):
        ms0[0, H0 + i, y0] = log_ref[i]
        ms0[1, H0 + i, y0] = stor_ref[i]
        pp[0, H0 + i, y0] = pert_ref[i]
        pp[1, H0 + i, y0] = press_ref[0, i]
        pp[2, H0 + i, y0] = press_ref[1, i]
    for i in range(CX1):
        ms1[0, H1 + i, y1] = halve(log_ref[2 * i], log_ref[2 * i + 1], CY1, 1)
        ms1[1, H1 + i, y1] = halve(stor_ref[2 * i], stor_ref[2 * i + 1], CY1, 1)
    for i in range(CX2):
        for f in range(2):
            ms2[f, H2 + i, y2] = halve(ms1[f, H1 + 2 * i, y1], ms1[f, H1 + 2 * i + 1, y1], CY2, 2)

    barrier = pltpu.get_barrier_semaphore()
    for dx, dy in WIDE:

        @pl.when(exists(dx, dy))
        def _():
            pl.semaphore_signal(
                barrier, inc=1, device_id=(gx + dx, gy + dy), device_id_type=MESH
            )

    beside_x = 1 + jnp.minimum(gx, 2) + jnp.minimum(gx_count - 1 - gx, 2)
    beside_y = 1 + jnp.minimum(gy, 1) + jnp.minimum(gy_count - 1 - gy, 1)
    pl.semaphore_wait(barrier, beside_x * beside_y - 1)

    setup = [
        copies(NEAR, s_ms0, views0s(ms0, W0)),
        copies(WIDE, s_ms2, views2s(ms2)),
        copies(NEAR, s_ms1, views1s(ms1)),
        copies(FACES, s_pp, views0s(pp, 1)),
    ]
    for made in setup:
        start(made)
    for made in setup:
        finish(made)

    def coefficients(ms, a, dinv, dg, factor, rows, core, halo, core_y, stride):
        ny = ms.shape[2]
        row = lax.broadcasted_iota(jnp.int32, (ny, NZ), 0) - HY + gy * core_y
        inside_y = jnp.logical_and(row >= 0, row < gy_count * core_y)
        lane = lax.broadcasted_iota(jnp.int32, (ny, NZ), 1)
        for i in rows:
            m = ms[0, i]
            total = ms[1, i]
            faces = []
            for other in (
                ms[0, i - 1],
                ms[0, i + 1],
                pltpu.roll(m, 1, 0),
                pltpu.roll(m, ny - 1, 0),
                pltpu.roll(m, stride, 1),
                pltpu.roll(m, NZ - stride, 1),
            ):
                faces.append(factor * jnp.exp(0.5 * (m + other)))
            faces[4] = jnp.where(lane >= stride, faces[4], 0.0)
            faces[5] = jnp.where(lane < NZ - stride, faces[5], 0.0)
            for face in faces:
                total = total + face
            place = gx * core + (i - halo)
            inside_x = jnp.logical_and(place >= 0, place < gx_count * core)
            scale = jnp.where(jnp.logical_and(inside_y, inside_x), OMEGA / total, 0.0)
            for f in range(6):
                a[f, i] = faces[f] * scale
            if halo <= i < halo + core:
                dinv[i - halo] = scale[HY : HY + core_y]
                if dg is not None:
                    dg[i - halo] = total[HY : HY + core_y] * (1.0 / OMEGA)

    coefficients(ms0, a0, dinv0, dg0, 1.0, range(1, NX0 - 1), CX0, H0, CY0, 1)
    coefficients(ms1, a1, dinv1, dg1, 0.25, range(1, NX1 - 1), CX1, H1, CY1, 2)
    coefficients(ms2, a2, dinv2, None, 0.0625, range(1, NX2 - 1), CX2, H2, CY2, 4)

    def relaxed(src, right, a, i, stride):
        ny = src.shape[0 if src.ndim == 2 else 1]
        c = src[i]
        new = (1.0 - OMEGA) * c + right
        new = new + a[0, i] * src[i - 1] + a[1, i] * src[i + 1]
        new = new + a[2, i] * pltpu.roll(c, 1, 0) + a[3, i] * pltpu.roll(c, ny - 1, 0)
        new = new + a[4, i] * pltpu.roll(c, stride, 1) + a[5, i] * pltpu.roll(c, NZ - stride, 1)
        return c, new

    def sweep(src, dst, right, a, rows, stride):
        for i in rows:
            dst[i] = relaxed(src, right(i), a, i, stride)[1]

    def around(core, halo, extra):
        return range(halo - extra, halo + core + extra)

    b1_right = lambda i: b1[i]
    b2_right = lambda i: b2[i]

    def neighbours(ref, lead, i):
        c = ref[lead, i] if lead is not None else ref[i]
        down = ref[lead, i - 1] if lead is not None else ref[i - 1]
        up = ref[lead, i + 1] if lead is not None else ref[i + 1]
        ny = c.shape[0]
        return c, (
            down,
            up,
            pltpu.roll(c, 1, 0),
            pltpu.roll(c, ny - 1, 0),
            pltpu.roll(c, 1, 1),
            pltpu.roll(c, NZ - 1, 1),
        )

    def solve(s, carry):
        slot = lax.rem(s, 2)

        @pl.when(s < TSTEPS)
        def _():
            for i in range(CX0):
                ext = H0 + i
                change, changes = neighbours(pp, 0, ext)
                press, presses = neighbours(pp, 1 + s, ext)
                total = jnp.zeros((NY0, NZ), F32)
                for f in range(6):
                    total = total + a0[f, ext] * (0.5 * (change + changes[f])) * (press - presses[f])
                bb[slot, ext, y0] = dinv0[i] * stor_ref[i] * prev[i] - total[HY : HY + CY0]

        @pl.when(s >= TSTEPS)
        def _():
            step = 2 * TSTEPS - 1 - s
            for i in range(CX0):
                bb[slot, H0 + i, y0] = dinv0[i] * (
                    stor_ref[i] * prev[i] + src_ref[step, i] * dps[step, i]
                )

        made = copies(NEAR, s_bb, views0(bb.at[slot], W0 - 1))
        start(made)
        xa[...] = jnp.zeros(xa.shape, F32)
        finish(made)
        bb_right = lambda i: bb[slot, i]

        def cycle(c, inner):
            sweep(xa, xb, bb_right, a0, around(CX0, H0, 2), 1)
            sweep(xb, xa, bb_right, a0, around(CX0, H0, 1), 1)
            for i in range(CX0):
                old, new = relaxed(xa, bb_right(H0 + i), a0, H0 + i, 1)
                r0[i] = (new - old)[HY : HY + CY0] * dg0[i]
            for i in range(CX1):
                b1[H1 + i, y1] = dinv1[i] * halve(r0[2 * i], r0[2 * i + 1], CY1, 1)
            made = copies(NEAR, s_b1, views1(b1))
            start(made)
            finish(made)
            sweep(b1, e1b, b1_right, a1, around(CX1, H1, 2), 2)
            for i in range(CX1):
                old, new = relaxed(e1b, b1[H1 + i], a1, H1 + i, 2)
                r1[i] = (new - old)[HY : HY + CY1] * dg1[i]
            for i in range(CX2):
                b2[H2 + i, y2] = dinv2[i] * halve(r1[2 * i], r1[2 * i + 1], CY2, 2)
            made = copies(WIDE, s_b2, views2(b2))
            start(made)
            finish(made)
            sweep(b2, e2a, b2_right, a2, around(CX2, H2, 3), 4)
            sweep(e2a, e2b, b2_right, a2, around(CX2, H2, 2), 4)
            sweep(e2b, e2a, b2_right, a2, around(CX2, H2, 1), 4)
            for j in range(CX2 + 2):
                spread = double(e2a[H2 - 1 + j, pl.ds(HY // 2, CY1)], CY1)
                low = H1 - 2 + 2 * j
                e1b[low] = e1b[low] + spread
                e1b[low + 1] = e1b[low + 1] + spread
            sweep(e1b, e1a, b1_right, a1, around(CX1, H1, 1), 2)
            for i in range(CX1):
                new = relaxed(e1a, b1[H1 + i], a1, H1 + i, 2)[1]
                spread = double(new[HY : HY + CY1], CY1)
                low = H0 + 2 * i
                xa[low, y0] = xa[low, y0] + spread
                xa[low + 1, y0] = xa[low + 1, y0] + spread
            made = copies(NEAR, s_x, views0(xa, W0))
            start(made)
            finish(made)
            sweep(xa, xb, bb_right, a0, around(CX0, H0, 4), 1)
            sweep(xb, xa, bb_right, a0, around(CX0, H0, 3), 1)
            return inner

        lax.fori_loop(0, VCYCLES, cycle, 0)

        @pl.when(s < TSTEPS)
        def _():
            for i in range(CX0):
                dps[s, i] = xa[H0 + i, y0]

        for i in range(CX0):
            prev[i] = jnp.where(s == TSTEPS - 1, 0.0, xa[H0 + i, y0])

        @pl.when(s >= TSTEPS)
        def _():
            step = 2 * TSTEPS - 1 - s
            for i in range(CX0):
                ext = H0 + i
                adjoint, adjoints = neighbours(xa, None, ext)
                press, presses = neighbours(pp, 1 + step, ext)
                total = jnp.zeros((NY0, NZ), F32)
                for f in range(6):
                    total = total + a0[f, ext] * (press - presses[f]) * (adjoint - adjoints[f])
                hess_ref[i] = hess_ref[i] - 0.5 * dg0[i] * total[HY : HY + CY0]

        return carry

    lax.fori_loop(0, 2 * TSTEPS, solve, 0)
    final_ref[...] = dps[TSTEPS - 1]


def gather_source(well_rows, well_cells, well_counts, well_owner, well_start, devices):
    sample_pos = jnp.arange(SAMPLES, dtype=jnp.int32)
    span = SAMPLES // TSTEPS
    counted = jnp.where(sample_pos[None, :] < well_counts[:, None], well_rows, 0.0)
    sums = []
    for step in range(TSTEPS):
        total = jnp.sum(counted[:, step * span : (step + 1) * span], axis=1)
        sums.append(jnp.where(step >= well_start, total, 0.0))
    owner = well_owner[:, 0]
    listed = owner.shape[0]
    position = jnp.arange(listed, dtype=jnp.int32)
    same = owner[:, None] == owner[None, :]
    earlier = position[None, :] < position[:, None]
    rank = jnp.sum(jnp.logical_and(same, earlier).astype(jnp.int32), axis=1)
    slot = owner * CAP + rank
    slots = devices * CAP
    hot = jnp.arange(slots, dtype=jnp.int32)[None, :] == slot[:, None]
    fields = [well_cells.astype(F32)] + sums
    send = jnp.stack(
        [jnp.sum(jnp.where(hot, field[:, None], 0.0), axis=0) for field in fields], axis=1
    )
    got = lax.all_to_all(send, ("gx", "gy"), split_axis=0, concat_axis=0, tiled=True)
    cell = got[:, 0].astype(jnp.int32)
    column = cell // NZ
    layer = cell % NZ
    columns = jnp.arange(CX0 * CY0, dtype=jnp.int32)[:, None] == column[None, :]
    layers = (jnp.arange(NZ, dtype=jnp.int32)[None, :] == layer[:, None]).astype(F32)
    weighted = jnp.stack(
        [jnp.where(columns, got[None, :, 1 + step], 0.0) for step in range(TSTEPS)]
    )
    placed = jnp.dot(
        weighted.reshape(TSTEPS * CX0 * CY0, slots), layers, precision=lax.Precision.HIGHEST
    )
    return placed.reshape(TSTEPS, CX0, CY0, NZ)


def local(
    log_perm,
    perturb,
    storage,
    base_press,
    well_rows,
    well_cells,
    well_counts,
    well_owner,
    well_start,
):
    gx_count = lax.axis_size("gx")
    gy_count = lax.axis_size("gy")
    source = gather_source(
        well_rows, well_cells, well_counts, well_owner, well_start, gx_count * gy_count
    )
    ext0 = (NX0, NY0, NZ)
    ext1 = (NX1, NY1, NZ)
    ext2 = (NX2, NY2, NZ)
    core0 = (CX0, CY0, NZ)
    core1 = (CX1, CY1, NZ)
    core2 = (CX2, CY2, NZ)

    def vmem(*shape):
        return pltpu.VMEM(shape, F32)

    def sems(count):
        return pltpu.SemaphoreType.DMA((2, count))

    spec = pl.BlockSpec(memory_space=pltpu.VMEM)

    def body(*refs):
        kernel(gx_count, gy_count, *refs)

    return pl.pallas_call(
        body,
        out_shape=(
            jax.ShapeDtypeStruct(core0, F32),
            jax.ShapeDtypeStruct(core0, F32),
        ),
        in_specs=[spec] * 5,
        out_specs=(spec, spec),
        scratch_shapes=[
            vmem(2, *ext0),
            vmem(2, *ext1),
            vmem(2, *ext2),
            vmem(3, *ext0),
            vmem(*ext0),
            vmem(*ext0),
            vmem(2, *ext0),
            vmem(6, *ext0),
            vmem(*core0),
            vmem(*core0),
            vmem(*core0),
            vmem(*ext1),
            vmem(*ext1),
            vmem(*ext1),
            vmem(6, *ext1),
            vmem(*core1),
            vmem(*core1),
            vmem(*core1),
            vmem(*ext2),
            vmem(*ext2),
            vmem(*ext2),
            vmem(6, *ext2),
            vmem(*core2),
            vmem(CY0, NZ),
            vmem(*core0),
            vmem(TSTEPS, *core0),
            sems(len(NEAR)),
            sems(len(NEAR)),
            sems(len(WIDE)),
            sems(len(FACES)),
            sems(len(NEAR)),
            sems(len(NEAR)),
            sems(len(NEAR)),
            sems(len(WIDE)),
        ],
        compiler_params=pltpu.CompilerParams(collective_id=0, has_side_effects=True),
    )(log_perm, perturb, storage, base_press, source)


def solution(mesh):
    return jax.shard_map(
        local,
        mesh=mesh,
        in_specs=(
            P("gx", "gy", None),
            P("gx", "gy", None),
            P("gx", "gy", None),
            P(None, "gx", "gy", None),
            P(("gx", "gy"), None),
            P(("gx", "gy")),
            P(("gx", "gy")),
            P(("gx", "gy"), None),
            P(("gx", "gy")),
        ),
        out_specs=(P("gx", "gy", None), P("gx", "gy", None)),
        check_vma=False,
    )
```

time: 1830 us -> 187 us (0.10); the launches traced: 1810 us -> 186 us
  starting transfers between devices: 1220 us -> 10.8 us
  waiting for transfers between devices: 355 us -> 8.77 us
  Pallas kernels: 0 us -> 156 us
  local copies, waits for them, and re-layouts: 141 us -> 6.48 us
  other arithmetic: 79.1 us -> 2.3 us
    ppermute x384 -> x0, starting transfers between devices: 1210 us -> none  [the longest x192 811 us: extended(): lax.ppermute(lax.slice_in_dim(block, block.shape[dim] - width, None, axis...]
    ppermute x384 -> x0, waiting for transfers between devices: 350 us -> none  [the longest x192 349 us: extended(): lax.ppermute(lax.slice_in_dim(block, block.shape[dim] - width, None, axis...]
    pallas_call x0 -> x1, Pallas kernels: none -> 156 us  [local(): pl.pallas_call(body, out_shape=(jax.ShapeDtypeStruct(core0, F32), jax.Sha...]
    reshape x50 -> x0, local copies, waits for them, and re-layouts: 111 us -> none  [the longest x18 107 us: coarsen(): values.reshape(size_x // 2, 2, size_y // 2, 2, size_z // 2, 2)]
    reduce_sum x22 -> x3, other arithmetic: 43.3 us -> 0.43 us  [the longest x1 0.17 us: gather_source(): rank = jnp.sum(jnp.logical_and(same, earlier).astype(jnp.int32), axis=1)]
    slice x129 -> x1, local copies, waits for them, and re-layouts: 21.4 us -> 0.12 us  [gather_source(): got[None, :, 1 + step]]
  transfers between devices with their start and end apart: 386 -> 1, of which waited for: 182 -> 1; matrix products, arithmetic and copies ran while one was open for 4% -> 0% of each run, Pallas kernels for 0% -> 0%
where the time goes in v1:
time: 187 us; the launch traced here: 186 us
  Pallas kernels  156 us (83%)
  starting transfers between devices  10.8 us (6%)
  waiting for transfers between devices  8.77 us (5%)
  local copies, waits for them, and re-layouts  6.48 us (3%)
  other arithmetic  2.3 us (1%)
    pallas_call x1, Pallas kernels, local(): pl.pallas_call(body, out_shape=(jax.ShapeDtypeStruct(core0, F32), jax.Sha...  156 us
    all_to_all x1, starting transfers between devices, gather_source(): lax.all_to_all(send, ('gx', 'gy'), split_axis=0, concat_axis=0, tiled=True)  10.8 us
    all_to_all x1, waiting for transfers between devices, gather_source(): lax.all_to_all(send, ('gx', 'gy'), split_axis=0, concat_axis=0, tiled=True)  8.77 us
    unnamed x13, local copies, waits for them, and re-layouts  4.44 us
  transfers between devices with their start and end apart: 1, of which 1 were waited for; matrix products, arithmetic and copies ran while one was open for 0% of the time, Pallas kernels for 0%

profile of v1, /device:TPU:3, one launch (start us, length us, event | category | flops | bytes accessed | tf_op | source)
XLA Modules:
  0.0 186.3 jit_solution(621199002834796884)
XLA Ops:
  0.6 0.7 convert_element_type.19
  1.3 0.7 copy-done.3
  1.9 0.2 convert_reduce_fusion
  2.1 0.0 copy-start.1
  2.1 0.6 copy-done.1
  2.8 1.0 fusion.4
  3.8 0.1 slice_reduce_fusion.1
  4.0 0.6 copy-done.2
  4.6 0.1 select_reduce_fusion.2
  4.8 0.1 stack.17
  4.9 0.1 stack.19
  5.0 0.1 stack.18
  5.2 1.5 copy.16
  6.7 10.8 %all-to-all-start = ((f32[128,2,3]{2,1,0:T(2,128)}), f32[128,2,3]{2,1,0:T(2,128)S(1)}, u32[]{:S(2)}, u32[]{:S(2)}) async-start(f32[128,2,3]{2,1,0:T(2,128)} %copy.16), calls=%async_computation | async-start | bytes 262144 | tf_op jit(solution)/shard_map/all_to_all | solution.py:438
  17.6 8.8 %all-to-all-done = f32[128,2,3]{2,1,0:T(2,128)S(1)} async-done(((f32[128,2,3]{2,1,0:T(2,128)}), f32[128,2,3]{2,1,0:T(2,128)S(1)}, u32[]{:S(2)}, u32[]{:S(2)}) %all-to-all-start) | async-done | bytes 3104 | tf_op jit(solution)/shard_map/all_to_all | solution.py:438
  26.3 0.1 fusion.12
  26.5 0.1 copy.20
  26.6 0.1 copy.21
  26.7 0.1 copy.22
  26.8 0.1 compare_select_fusion.1
  26.9 1.1 fusion.refs_4_
  28.0 156.0 %shard_map.104 = (f32[8,32,128]{2,1,0:T(8,128)}, f32[8,32,128]{2,1,0:T(8,128)}) custom-call(f32[8,32,128]{2,1,0:T(8,128)} %refs_0_.1, f32[8,32,128]{2,1,0:T(8,128)} %refs_1_.1, f32[8,32,128]{2,1,0:T(8,128)} %refs_2_.1, f32[2,8,32,128]{3,2,1,0:T(8,128)} %refs_3_.1, f32[2,8,32,128]{3,2,1,0:T(8,128)} %fusion.refs_4_), custom_call_target="tpu_custom_call" | custom-call | tf_op jit(solution)/shard_map/pallas_call | solution.py:487
  184.0 1.6 copy.25
  185.6 0.7 copy.26
  (11 shorter events, 0.1 us)
Async XLA Ops:
  1.3 0.7 copy-start.3
  2.1 0.7 copy-start.1
  3.9 0.7 copy-start.2
  6.7 19.6 %all-to-all-start = ((f32[128,2,3]{2,1,0:T(2,128)}), f32[128,2,3]{2,1,0:T(2,128)S(1)}, u32[]{:S(2)}, u32[]{:S(2)}) async-start(f32[128,2,3]{2,1,0:T(2,128)} %copy.16), calls=%async_computation | async-start | bytes 262144 | tf_op jit(solution)/shard_map/all_to_all | solution.py:438
  184.0 1.6 copy-start

commit v2 on v1

--- a/solution.py
+++ b/solution.py
@@ -58,6 +58,57 @@
     )
 
 
+def list_wells(rows_ref, ints_ref, listed):
+    wells = rows_ref.shape[0]
+    lane = lax.broadcasted_iota(jnp.int32, (wells, NZ), 1).astype(F32)
+    well = lax.broadcasted_iota(jnp.int32, (wells, NZ), 0).astype(F32)
+    across = [
+        jnp.broadcast_to(ints_ref[pl.ds(k, 1), :].astype(F32), (NZ, wells)) for k in range(4)
+    ]
+    cell, count, owner, begin = [jnp.transpose(values) for values in across]
+    fields = [cell]
+    span = SAMPLES // TSTEPS
+    for step in range(TSTEPS):
+        total = jnp.zeros((wells, NZ), F32)
+        for first in range(step * span, (step + 1) * span, NZ):
+            records = rows_ref[:, pl.ds(first, NZ)]
+            total = total + jnp.where(lane + float(first) < count, records, 0.0)
+        total = jnp.sum(total, axis=1, keepdims=True)
+        fields.append(jnp.where(begin <= float(step), total, 0.0))
+    earlier = jnp.logical_and(owner == across[2], lane < well)
+    rank = jnp.sum(jnp.where(earlier, 1.0, 0.0), axis=1, keepdims=True)
+    listed[...] = jnp.zeros(listed.shape, F32)
+    for slot in range(CAP):
+        hit = jnp.logical_and(owner == lane, rank == float(slot))
+        for f, field in enumerate(fields):
+            listed[pl.ds(3 * slot + f, 1), :] = jnp.sum(
+                jnp.where(hit, field, 0.0), axis=0, keepdims=True
+            )
+
+
+def place_wells(table, src_ref):
+    columns = CX0 * CY0
+    column = lax.broadcasted_iota(jnp.int32, (columns, NZ), 0)
+    layer = lax.broadcasted_iota(jnp.int32, (NZ, NZ), 0)
+    placed = [None] * TSTEPS
+    for slot in range(CAP):
+        cell = table[3 * slot : 3 * slot + 1].astype(jnp.int32)
+        here = column == cell // NZ
+        deep = jnp.where(layer == lax.rem(cell, NZ), 1.0, 0.0)
+        for step in range(TSTEPS):
+            weight = table[3 * slot + 1 + step : 3 * slot + 2 + step]
+            part = lax.dot_general(
+                jnp.where(here, weight, 0.0),
+                deep,
+                (((1,), (1,)), ((), ())),
+                precision=lax.Precision.HIGHEST,
+                preferred_element_type=F32,
+            )
+            placed[step] = part if placed[step] is None else placed[step] + part
+    for step in range(TSTEPS):
+        src_ref[step] = placed[step].reshape(CX0, CY0, NZ)
+
+
 def kernel(
     gx_count,
     gy_count,
@@ -65,7 +116,8 @@
     pert_ref,
     stor_ref,
     press_ref,
-    src_ref,
+    rows_ref,
+    ints_ref,
     hess_ref,
     final_ref,
     ms0,
@@ -94,6 +146,11 @@
     pair,
     prev,
     dps,
+    listed,
+    by_row,
+    sorted_ref,
+    by_col,
+    src_ref,
     s_ms0,
     s_ms1,
     s_ms2,
@@ -102,6 +159,8 @@
     s_x,
     s_b1,
     s_b2,
+    s_row,
+    s_col,
 ):
     gx = lax.axis_index("gx")
     gy = lax.axis_index("gy")
@@ -146,6 +205,19 @@
         for dx, dy, copy in made:
             pl.when(exists(dx, dy))(copy.wait_send)
 
+    def spread(table, slots, sems, peers):
+        return [
+            pltpu.make_async_remote_copy(
+                src_ref=table,
+                dst_ref=slots.at[k],
+                send_sem=sems.at[0, k],
+                recv_sem=sems.at[1, k],
+                device_id=peer,
+                device_id_type=MESH,
+            )
+            for k, peer in enumerate(peers)
+        ]
+
     def views0(ref, width):
         def at(dx, dy):
             sx, tx = span_x(dx, CX0, H0, width)
@@ -223,18 +295,24 @@
         for f in range(2):
             ms2[f, H2 + i, y2] = halve(ms1[f, H1 + 2 * i, y1], ms1[f, H1 + 2 * i + 1, y1], CY2, 2)
 
+    row_peers = [(lax.rem(gx + k, gx_count), gy) for k in range(1, gx_count)]
+    col_peers = [(gx, lax.rem(gy + k, gy_count)) for k in range(1, gy_count)]
+
     barrier = pltpu.get_barrier_semaphore()
+    for peer in row_peers + col_peers:
+        pl.semaphore_signal(barrier, inc=1, device_id=peer, device_id_type=MESH)
     for dx, dy in WIDE:
-
-        @pl.when(exists(dx, dy))
-        def _():
-            pl.semaphore_signal(
-                barrier, inc=1, device_id=(gx + dx, gy + dy), device_id_type=MESH
-            )
-
-    beside_x = 1 + jnp.minimum(gx, 2) + jnp.minimum(gx_count - 1 - gx, 2)
-    beside_y = 1 + jnp.minimum(gy, 1) + jnp.minimum(gy_count - 1 - gy, 1)
-    pl.semaphore_wait(barrier, beside_x * beside_y - 1)
+        if dx != 0 and dy != 0:
+
+            @pl.when(exists(dx, dy))
+            def _():
+                pl.semaphore_signal(
+                    barrier, inc=1, device_id=(gx + dx, gy + dy), device_id_type=MESH
+                )
+
+    beside_x = jnp.minimum(gx, 2) + jnp.minimum(gx_count - 1 - gx, 2)
+    beside_y = jnp.minimum(gy, 1) + jnp.minimum(gy_count - 1 - gy, 1)
+    pl.semaphore_wait(barrier, beside_x * beside_y + gx_count - 1 + gy_count - 1)
 
     setup = [
         copies(NEAR, s_ms0, views0s(ms0, W0)),
@@ -244,6 +322,10 @@
     ]
     for made in setup:
         start(made)
+    list_wells(rows_ref, ints_ref, listed)
+    row_copies = spread(listed, by_row, s_row, row_peers)
+    for copy in row_copies:
+        copy.start()
     for made in setup:
         finish(made)
 
@@ -315,6 +397,8 @@
             pltpu.roll(c, 1, 1),
             pltpu.roll(c, NZ - 1, 1),
         )
+
+    col_copies = spread(sorted_ref, by_col, s_col, col_peers)
 
     def solve(s, carry):
         slot = lax.rem(s, 2)
@@ -393,6 +477,36 @@
             for i in range(CX0):
                 dps[s, i] = xa[H0 + i, y0]
 
+        @pl.when(s == 0)
+        def _():
+            for copy in row_copies:
+                copy.wait()
+            lane = lax.broadcasted_iota(jnp.int32, (8, NZ), 1)
+            total = jnp.zeros((8, NZ), F32)
+            for k in range(gx_count):
+                table = listed[...] if k == 0 else by_row[k - 1]
+                owned = jnp.where(lane // gy_count == gx, table, 0.0)
+                sender = lax.rem(gx + gx_count - k, gx_count)
+                shift = lax.rem((sender - gx + gx_count) * gy_count, NZ)
+                total = total + pltpu.roll(owned, shift, 1)
+            sorted_ref[...] = total
+            for copy in col_copies:
+                copy.start()
+
+        @pl.when(s == TSTEPS - 1)
+        def _():
+            for copy in col_copies:
+                copy.wait()
+            lane = lax.broadcasted_iota(jnp.int32, (8, NZ), 1)
+            mine = lax.rem(lane, gy_count) == gy
+            total = jnp.zeros((8, NZ), F32)
+            for k in range(gy_count):
+                table = sorted_ref[...] if k == 0 else by_col[k - 1]
+                sender = lax.rem(gy + gy_count - k, gy_count)
+                shift = lax.rem(sender - gy + NZ, NZ)
+                total = total + pltpu.roll(jnp.where(mine, table, 0.0), shift, 1)
+            place_wells(total, src_ref)
+
         for i in range(CX0):
             prev[i] = jnp.where(s == TSTEPS - 1, 0.0, xa[H0 + i, y0])
 
@@ -412,42 +526,6 @@
 
     lax.fori_loop(0, 2 * TSTEPS, solve, 0)
     final_ref[...] = dps[TSTEPS - 1]
-
-
-def gather_source(well_rows, well_cells, well_counts, well_owner, well_start, devices):
-    sample_pos = jnp.arange(SAMPLES, dtype=jnp.int32)
-    span = SAMPLES // TSTEPS
-    counted = jnp.where(sample_pos[None, :] < well_counts[:, None], well_rows, 0.0)
-    sums = []
-    for step in range(TSTEPS):
-        total = jnp.sum(counted[:, step * span : (step + 1) * span], axis=1)
-        sums.append(jnp.where(step >= well_start, total, 0.0))
-    owner = well_owner[:, 0]
-    listed = owner.shape[0]
-    position = jnp.arange(listed, dtype=jnp.int32)
-    same = owner[:, None] == owner[None, :]
-    earlier = position[None, :] < position[:, None]
-    rank = jnp.sum(jnp.logical_and(same, earlier).astype(jnp.int32), axis=1)
-    slot = owner * CAP + rank
-    slots = devices * CAP
-    hot = jnp.arange(slots, dtype=jnp.int32)[None, :] == slot[:, None]
-    fields = [well_cells.astype(F32)] + sums
-    send = jnp.stack(
-        [jnp.sum(jnp.where(hot, field[:, None], 0.0), axis=0) for field in fields], axis=1
-    )
-    got = lax.all_to_all(send, ("gx", "gy"), split_axis=0, concat_axis=0, tiled=True)
-    cell = got[:, 0].astype(jnp.int32)
-    column = cell // NZ
-    layer = cell % NZ
-    columns = jnp.arange(CX0 * CY0, dtype=jnp.int32)[:, None] == column[None, :]
-    layers = (jnp.arange(NZ, dtype=jnp.int32)[None, :] == layer[:, None]).astype(F32)
-    weighted = jnp.stack(
-        [jnp.where(columns, got[None, :, 1 + step], 0.0) for step in range(TSTEPS)]
-    )
-    placed = jnp.dot(
-        weighted.reshape(TSTEPS * CX0 * CY0, slots), layers, precision=lax.Precision.HIGHEST
-    )
-    return placed.reshape(TSTEPS, CX0, CY0, NZ)
 
 
 def local(
@@ -463,9 +541,7 @@
 ):
     gx_count = lax.axis_size("gx")
     gy_count = lax.axis_size("gy")
-    source = gather_source(
-        well_rows, well_cells, well_counts, well_owner, well_start, gx_count * gy_count
-    )
+    ints = jnp.stack([well_cells, well_counts, well_owner[:, 0], well_start])
     ext0 = (NX0, NY0, NZ)
     ext1 = (NX1, NY1, NZ)
     ext2 = (NX2, NY2, NZ)
@@ -490,7 +566,7 @@
             jax.ShapeDtypeStruct(core0, F32),
             jax.ShapeDtypeStruct(core0, F32),
         ),
-        in_specs=[spec] * 5,
+        in_specs=[spec] * 6,
         out_specs=(spec, spec),
         scratch_shapes=[
             vmem(2, *ext0),
@@ -519,6 +595,11 @@
             vmem(CY0, NZ),
             vmem(*core0),
             vmem(TSTEPS, *core0),
+            vmem(8, NZ),
+            vmem(gx_count - 1, 8, NZ),
+            vmem(8, NZ),
+            vmem(gy_count - 1, 8, NZ),
+            vmem(TSTEPS, *core0),
             sems(len(NEAR)),
             sems(len(NEAR)),
             sems(len(WIDE)),
@@ -527,9 +608,11 @@
             sems(len(NEAR)),
             sems(len(NEAR)),
             sems(len(WIDE)),
+            sems(gx_count - 1),
+            sems(gy_count - 1),
         ],
         compiler_params=pltpu.CompilerParams(collective_id=0, has_side_effects=True),
-    )(log_perm, perturb, storage, base_press, source)
+    )(log_perm, perturb, storage, base_press, well_rows, ints)
 
 
 def solution(mesh):

time: 187 us -> 165 us (0.88)
  starting transfers between devices: 10.8 us -> 0 us
  waiting for transfers between devices: 8.77 us -> 0 us
  Pallas kernels: 156 us -> 161 us
  local copies, waits for them, and re-layouts: 6.48 us -> 2.93 us
    all_to_all x1 -> x0, starting transfers between devices: 10.8 us -> none  [gather_source(): lax.all_to_all(send, ('gx', 'gy'), split_axis=0, concat_axis=0, tiled=True)]
    all_to_all x1 -> x0, waiting for transfers between devices: 8.77 us -> none  [gather_source(): lax.all_to_all(send, ('gx', 'gy'), split_axis=0, concat_axis=0, tiled=True)]
    pallas_call x1, Pallas kernels: 156 us -> 161 us  [local(): pl.pallas_call(body, out_shape=(jax.ShapeDtypeStruct(core0, F32), jax.Sha...]
    another operation x4 -> x0, local copies, waits for them, and re-layouts: 1.91 us -> none  [gather_source(): jnp.stack([jnp.sum(jnp.where(hot, field[:, None], 0.0), axis=0) for field...]
    unnamed x13 -> x12, local copies, waits for them, and re-layouts: 4.44 us -> 2.93 us
  transfers between devices with their start and end apart: 1 -> 0, of which waited for: 1 -> 0; matrix products, arithmetic and copies ran while one was open for 0% -> 0% of each run, Pallas kernels for 0% -> 0%
where the time goes in v2:
time: 165 us
  Pallas kernels  161 us (98%)
  local copies, waits for them, and re-layouts  2.93 us (2%)
    pallas_call x1, Pallas kernels, local(): pl.pallas_call(body, out_shape=(jax.ShapeDtypeStruct(core0, F32), jax.Sha...  161 us

profile of v2, /device:TPU:3, one launch (start us, length us, event | category | flops | bytes accessed | tf_op | source)
XLA Modules:
  0.0 165.1 jit_solution(10978223348301549578)
XLA Ops:
  0.6 0.0 copy-start.4
  0.6 0.0 copy-start.1
  0.7 0.0 copy-start.2
  0.7 0.0 copy-start.3
  0.7 0.6 copy-done.4
  1.3 0.0 copy-done.1
  1.3 0.0 copy-done.2
  1.3 0.0 copy-done.3
  1.3 0.6 pad_add_fusion.refs_5_
  1.9 160.9 %shard_map.104 = (f32[8,32,128]{2,1,0:T(8,128)}, f32[8,32,128]{2,1,0:T(8,128)}) custom-call(f32[8,32,128]{2,1,0:T(8,128)} %refs_0_.1, f32[8,32,128]{2,1,0:T(8,128)} %refs_1_.1, f32[8,32,128]{2,1,0:T(8,128)} %refs_2_.1, f32[2,8,32,128]{3,2,1,0:T(8,128)} %refs_3_.1, f32[128,512]{1,0:T(8,128)} %refs_4_.1, s32[4,128]{1,0:T(4,128)} %pad_add_fusion.refs_5_), custom_call_target="tpu_custom_call" | custom-call | tf_op jit(solution)/shard_map/pallas_call | solution.py:563
  162.9 0.0 copy-start
  162.9 1.6 copy.13
  164.5 0.0 copy-done
  164.5 0.7 copy.14
Async XLA Ops:
  0.6 0.7 copy-start.4
  0.6 0.7 copy-start.1
  0.7 0.7 copy-start.2
  0.7 0.7 copy-start.3
  162.9 1.6 copy-start

commit v3 on v2

--- a/solution.py
+++ b/solution.py
@@ -23,9 +23,13 @@
 NX2, NY2 = CX2 + 2 * H2, CY2 + 2 * HY
 NZ = 128
 
-NEAR = [(dx, dy) for dx in (-1, 0, 1) for dy in (-1, 0, 1) if (dx, dy) != (0, 0)]
-FACES = [(-1, 0), (1, 0), (0, -1), (0, 1)]
-WIDE = [(dx, dy) for dx in (-2, -1, 0, 1, 2) for dy in (-1, 0, 1) if (dx, dy) != (0, 0)]
+
+def ordered(offsets):
+    return sorted(offsets, key=lambda o: (o[1] == 0, -abs(o[0]), o))
+
+
+NEAR = ordered([(dx, dy) for dx in (-1, 0, 1) for dy in (-1, 0, 1) if (dx, dy) != (0, 0)])
+WIDE = ordered([(dx, dy) for dx in (-2, -1, 0, 1, 2) for dy in (-1, 0, 1) if (dx, dy) != (0, 0)])
 
 
 def span_x(dx, core, halo, width):
@@ -36,16 +40,38 @@
     return pl.ds(halo, core), pl.ds(halo, core)
 
 
-def span_y(dy, core):
+def span_y(dy, core, width):
     if dy > 0:
-        return pl.ds(core, HY), pl.ds(0, HY)
+        return pl.ds(HY + core - width, width), pl.ds(HY - width, width)
     if dy < 0:
-        return pl.ds(HY, HY), pl.ds(HY + core, HY)
+        return pl.ds(HY, width), pl.ds(HY + core, width)
     return pl.ds(HY, core), pl.ds(HY, core)
 
 
-def span_tile(dx):
-    return pl.ds(H2, CX2), pl.ds(H2 - CX2 * dx, CX2)
+def strips(ref, core_x, halo, width, core_y):
+    def at(dx, dy):
+        if dx != 0 and dy != 0:
+            deep, rows = width - 1, 4 * -(-(width - 1) // 4)
+        else:
+            deep, rows = width, 4 * -(-width // 4)
+        sx, tx = span_x(dx, core_x, halo, deep)
+        sy, ty = span_y(dy, core_y, rows)
+        if len(ref.shape) == 4:
+            return ref.at[:, sx, sy], ref.at[:, tx, ty]
+        return ref.at[sx, sy], ref.at[tx, ty]
+
+    return at
+
+
+def tiles(ref):
+    def at(dx, dy):
+        sx, tx = pl.ds(H2, CX2), pl.ds(H2 - CX2 * dx, CX2)
+        sy, ty = span_y(dy, CY2, 4)
+        if len(ref.shape) == 4:
+            return ref.at[:, sx, sy], ref.at[:, tx, ty]
+        return ref.at[sx, sy], ref.at[tx, ty]
+
+    return at
 
 
 def swap_pair(values, stride):
@@ -106,7 +132,7 @@
             )
             placed[step] = part if placed[step] is None else placed[step] + part
     for step in range(TSTEPS):
-        src_ref[step] = placed[step].reshape(CX0, CY0, NZ)
+        src_ref[step, pl.ds(H0, CX0), pl.ds(HY, CY0)] = placed[step].reshape(CX0, CY0, NZ)
 
 
 def kernel(
@@ -144,7 +170,7 @@
     a2,
     dinv2,
     pair,
-    prev,
+    bl,
     dps,
     listed,
     by_row,
@@ -161,6 +187,7 @@
     s_b2,
     s_row,
     s_col,
+    s_src,
 ):
     gx = lax.axis_index("gx")
     gy = lax.axis_index("gy")
@@ -218,53 +245,11 @@
             for k, peer in enumerate(peers)
         ]
 
-    def views0(ref, width):
-        def at(dx, dy):
-            sx, tx = span_x(dx, CX0, H0, width)
-            sy, ty = span_y(dy, CY0)
-            return ref.at[sx, sy], ref.at[tx, ty]
-
-        return at
-
-    def views0s(ref, width):
-        def at(dx, dy):
-            sx, tx = span_x(dx, CX0, H0, width)
-            sy, ty = span_y(dy, CY0)
-            return ref.at[:, sx, sy], ref.at[:, tx, ty]
-
-        return at
-
-    def views1(ref):
-        def at(dx, dy):
-            sx, tx = span_x(dx, CX1, H1, W1)
-            sy, ty = span_y(dy, CY1)
-            return ref.at[sx, sy], ref.at[tx, ty]
-
-        return at
-
-    def views1s(ref):
-        def at(dx, dy):
-            sx, tx = span_x(dx, CX1, H1, W1)
-            sy, ty = span_y(dy, CY1)
-            return ref.at[:, sx, sy], ref.at[:, tx, ty]
-
-        return at
-
-    def views2(ref):
-        def at(dx, dy):
-            sx, tx = span_tile(dx)
-            sy, ty = span_y(dy, CY2)
-            return ref.at[sx, sy], ref.at[tx, ty]
-
-        return at
-
-    def views2s(ref):
-        def at(dx, dy):
-            sx, tx = span_tile(dx)
-            sy, ty = span_y(dy, CY2)
-            return ref.at[:, sx, sy], ref.at[:, tx, ty]
-
-        return at
+    def fine(ref, width):
+        return strips(ref, CX0, H0, width, CY0)
+
+    def middle(ref):
+        return strips(ref, CX1, H1, W1, CY1)
 
     def halve(first, second, size, stride):
         pair[pl.ds(0, 2 * size), :] = first + second
@@ -278,9 +263,8 @@
 
     y0, y1, y2 = pl.ds(HY, CY0), pl.ds(HY, CY1), pl.ds(HY, CY2)
 
-    for ref in (ms0, ms1, ms2, pp, xa, xb, bb, b1, e1a, e1b, b2, e2a, e2b, a0, a1, a2):
+    for ref in (ms0, ms1, ms2, pp, xa, xb, bb, b1, e1a, e1b, b2, e2a, e2b, a0, a1, a2, bl, dps, src_ref, dinv0):
         ref[...] = jnp.zeros(ref.shape, F32)
-    prev[...] = jnp.zeros(prev.shape, F32)
     hess_ref[...] = jnp.zeros(hess_ref.shape, F32)
     for i in range(CX0):
         ms0[0, H0 + i, y0] = log_ref[i]
@@ -315,10 +299,10 @@
     pl.semaphore_wait(barrier, beside_x * beside_y + gx_count - 1 + gy_count - 1)
 
     setup = [
-        copies(NEAR, s_ms0, views0s(ms0, W0)),
-        copies(WIDE, s_ms2, views2s(ms2)),
-        copies(NEAR, s_ms1, views1s(ms1)),
-        copies(FACES, s_pp, views0s(pp, 1)),
+        copies(NEAR, s_ms0, fine(ms0, W0)),
+        copies(WIDE, s_ms2, tiles(ms2)),
+        copies(NEAR, s_ms1, middle(ms1)),
+        copies(NEAR, s_pp, fine(pp, 3)),
     ]
     for made in setup:
         start(made)
@@ -356,8 +340,11 @@
             scale = jnp.where(jnp.logical_and(inside_y, inside_x), OMEGA / total, 0.0)
             for f in range(6):
                 a[f, i] = faces[f] * scale
+            if core == CX0:
+                dinv[i] = scale
+            elif halo <= i < halo + core:
+                dinv[i - halo] = scale[HY : HY + core_y]
             if halo <= i < halo + core:
-                dinv[i - halo] = scale[HY : HY + core_y]
                 if dg is not None:
                     dg[i - halo] = total[HY : HY + core_y] * (1.0 / OMEGA)
 
@@ -381,6 +368,7 @@
     def around(core, halo, extra):
         return range(halo - extra, halo + core + extra)
 
+    bb_right = lambda i: bl[i]
     b1_right = lambda i: b1[i]
     b2_right = lambda i: b2[i]
 
@@ -399,34 +387,29 @@
         )
 
     col_copies = spread(sorted_ref, by_col, s_col, col_peers)
+    src_copies = copies(NEAR, s_src, fine(src_ref, 2))
 
     def solve(s, carry):
-        slot = lax.rem(s, 2)
-
         @pl.when(s < TSTEPS)
         def _():
-            for i in range(CX0):
-                ext = H0 + i
-                change, changes = neighbours(pp, 0, ext)
-                press, presses = neighbours(pp, 1 + s, ext)
-                total = jnp.zeros((NY0, NZ), F32)
+            for i in around(CX0, H0, 2):
+                change, changes = neighbours(pp, 0, i)
+                press, presses = neighbours(pp, 1 + s, i)
+                total = dinv0[i] * (ms0[1, i] * xa[i])
                 for f in range(6):
-                    total = total + a0[f, ext] * (0.5 * (change + changes[f])) * (press - presses[f])
-                bb[slot, ext, y0] = dinv0[i] * stor_ref[i] * prev[i] - total[HY : HY + CY0]
+                    total = total - a0[f, i] * (0.5 * (change + changes[f])) * (press - presses[f])
+                bl[i] = total
 
         @pl.when(s >= TSTEPS)
         def _():
             step = 2 * TSTEPS - 1 - s
-            for i in range(CX0):
-                bb[slot, H0 + i, y0] = dinv0[i] * (
-                    stor_ref[i] * prev[i] + src_ref[step, i] * dps[step, i]
-                )
-
-        made = copies(NEAR, s_bb, views0(bb.at[slot], W0 - 1))
-        start(made)
+            for i in around(CX0, H0, 2):
+                bl[i] = dinv0[i] * (ms0[1, i] * xa[i] + src_ref[step, i] * dps[step, i])
+
+        for i in around(CX0, H0, 0):
+            bb[i, y0] = bl[i, y0]
         xa[...] = jnp.zeros(xa.shape, F32)
-        finish(made)
-        bb_right = lambda i: bb[slot, i]
+        bb_copies = copies(NEAR, s_bb, fine(bb, W0 - 1))
 
         def cycle(c, inner):
             sweep(xa, xb, bb_right, a0, around(CX0, H0, 2), 1)
@@ -436,8 +419,13 @@
                 r0[i] = (new - old)[HY : HY + CY0] * dg0[i]
             for i in range(CX1):
                 b1[H1 + i, y1] = dinv1[i] * halve(r0[2 * i], r0[2 * i + 1], CY1, 1)
-            made = copies(NEAR, s_b1, views1(b1))
+            made = copies(NEAR, s_b1, middle(b1))
             start(made)
+
+            @pl.when(c == 0)
+            def _():
+                start(bb_copies)
+
             finish(made)
             sweep(b1, e1b, b1_right, a1, around(CX1, H1, 2), 2)
             for i in range(CX1):
@@ -445,7 +433,7 @@
                 r1[i] = (new - old)[HY : HY + CY1] * dg1[i]
             for i in range(CX2):
                 b2[H2 + i, y2] = dinv2[i] * halve(r1[2 * i], r1[2 * i + 1], CY2, 2)
-            made = copies(WIDE, s_b2, views2(b2))
+            made = copies(WIDE, s_b2, tiles(b2))
             start(made)
             finish(made)
             sweep(b2, e2a, b2_right, a2, around(CX2, H2, 3), 4)
@@ -463,9 +451,53 @@
                 low = H0 + 2 * i
                 xa[low, y0] = xa[low, y0] + spread
                 xa[low + 1, y0] = xa[low + 1, y0] + spread
-            made = copies(NEAR, s_x, views0(xa, W0))
+            made = copies(NEAR, s_x, fine(xa, W0))
             start(made)
+            turn = s * VCYCLES + c
+
+            @pl.when(turn == 0)
+            def _():
+                for copy in row_copies:
+                    copy.wait()
+                lane = lax.broadcasted_iota(jnp.int32, (8, NZ), 1)
+                total = jnp.zeros((8, NZ), F32)
+                for k in range(gx_count):
+                    table = listed[...] if k == 0 else by_row[k - 1]
+                    owned = jnp.where(lane // gy_count == gx, table, 0.0)
+                    sender = lax.rem(gx + gx_count - k, gx_count)
+                    shift = lax.rem((sender - gx + gx_count) * gy_count, NZ)
+                    total = total + pltpu.roll(owned, shift, 1)
+                sorted_ref[...] = total
+                for copy in col_copies:
+                    copy.start()
+
+            @pl.when(turn == 1)
+            def _():
+                for copy in col_copies:
+                    copy.wait()
+                lane = lax.broadcasted_iota(jnp.int32, (8, NZ), 1)
+                mine = lax.rem(lane, gy_count) == gy
+                total = jnp.zeros((8, NZ), F32)
+                for k in range(gy_count):
+                    table = sorted_ref[...] if k == 0 else by_col[k - 1]
+                    sender = lax.rem(gy + gy_count - k, gy_count)
+                    shift = lax.rem(sender - gy + NZ, NZ)
+                    total = total + pltpu.roll(jnp.where(mine, table, 0.0), shift, 1)
+                place_wells(total, src_ref)
+                start(src_copies)
+
+            @pl.when(turn == 3)
+            def _():
+                finish(src_copies)
+
             finish(made)
+
+            @pl.when(c == 0)
+            def _():
+                finish(bb_copies)
+                for i in around(CX0, H0, 4):
+                    bl[i] = bb[i]
+
             sweep(xa, xb, bb_right, a0, around(CX0, H0, 4), 1)
             sweep(xb, xa, bb_right, a0, around(CX0, H0, 3), 1)
             return inner
@@ -474,41 +506,13 @@
 
         @pl.when(s < TSTEPS)
         def _():
-            for i in range(CX0):
-                dps[s, i] = xa[H0 + i, y0]
-
-        @pl.when(s == 0)
-        def _():
-            for copy in row_copies:
-                copy.wait()
-            lane = lax.broadcasted_iota(jnp.int32, (8, NZ), 1)
-            total = jnp.zeros((8, NZ), F32)
-            for k in range(gx_count):
-                table = listed[...] if k == 0 else by_row[k - 1]
-                owned = jnp.where(lane // gy_count == gx, table, 0.0)
-                sender = lax.rem(gx + gx_count - k, gx_count)
-                shift = lax.rem((sender - gx + gx_count) * gy_count, NZ)
-                total = total + pltpu.roll(owned, shift, 1)
-            sorted_ref[...] = total
-            for copy in col_copies:
-                copy.start()
+            for i in around(CX0, H0, 2):
+                dps[s, i] = xa[i]
 
         @pl.when(s == TSTEPS - 1)
         def _():
-            for copy in col_copies:
-                copy.wait()
-            lane = lax.broadcasted_iota(jnp.int32, (8, NZ), 1)
-            mine = lax.rem(lane, gy_count) == gy
-            total = jnp.zeros((8, NZ), F32)
-            for k in range(gy_count):
-                table = sorted_ref[...] if k == 0 else by_col[k - 1]
-                sender = lax.rem(gy + gy_count - k, gy_count)
-                shift = lax.rem(sender - gy + NZ, NZ)
-                total = total + pltpu.roll(jnp.where(mine, table, 0.0), shift, 1)
-            place_wells(total, src_ref)
-
-        for i in range(CX0):
-            prev[i] = jnp.where(s == TSTEPS - 1, 0.0, xa[H0 + i, y0])
+            final_ref[...] = xa[pl.ds(H0, CX0), y0]
+            xa[...] = jnp.zeros(xa.shape, F32)
 
         @pl.when(s >= TSTEPS)
         def _():
@@ -525,7 +529,6 @@
         return carry
 
     lax.fori_loop(0, 2 * TSTEPS, solve, 0)
-    final_ref[...] = dps[TSTEPS - 1]
 
 
 def local(
@@ -575,9 +578,9 @@
             vmem(3, *ext0),
             vmem(*ext0),
             vmem(*ext0),
-            vmem(2, *ext0),
+            vmem(*ext0),
             vmem(6, *ext0),
-            vmem(*core0),
+            vmem(*ext0),
             vmem(*core0),
             vmem(*core0),
             vmem(*ext1),
@@ -593,23 +596,24 @@
             vmem(6, *ext2),
             vmem(*core2),
             vmem(CY0, NZ),
-            vmem(*core0),
-            vmem(TSTEPS, *core0),
+            vmem(*ext0),
+            vmem(TSTEPS, *ext0),
             vmem(8, NZ),
             vmem(gx_count - 1, 8, NZ),
             vmem(8, NZ),
             vmem(gy_count - 1, 8, NZ),
-            vmem(TSTEPS, *core0),
+            vmem(TSTEPS, *ext0),
             sems(len(NEAR)),
             sems(len(NEAR)),
             sems(len(WIDE)),
-            sems(len(FACES)),
+            sems(len(NEAR)),
             sems(len(NEAR)),
             sems(len(NEAR)),
             sems(len(NEAR)),
             sems(len(WIDE)),
             sems(gx_count - 1),
             sems(gy_count - 1),
+            sems(len(NEAR)),
         ],
         compiler_params=pltpu.CompilerParams(collective_id=0, has_side_effects=True),
     )(log_perm, perturb, storage, base_press, well_rows, ints)

time: 165 us -> 139 us (0.84)
  Pallas kernels: 161 us -> 134 us
    pallas_call x1, Pallas kernels: 161 us -> 134 us  [local(): pl.pallas_call(body, out_shape=(jax.ShapeDtypeStruct(core0, F32), jax.Sha...]
where the time goes in v3:
time: 139 us; the launch traced here: 138 us
  Pallas kernels  134 us (96%)
  local copies, waits for them, and re-layouts  2.93 us (2%)
    pallas_call x1, Pallas kernels, local(): pl.pallas_call(body, out_shape=(jax.ShapeDtypeStruct(core0, F32), jax.Sha...  134 us
    unnamed x12, local copies, waits for them, and re-layouts  2.93 us

profile of v3, /device:TPU:3, one launch (start us, length us, event | category | flops | bytes accessed | tf_op | source)
XLA Modules:
  0.0 138.4 jit_solution(16799755582867566222)
XLA Ops:
  0.6 0.0 copy-start.4
  0.6 0.0 copy-start.1
  0.7 0.0 copy-start.2
  0.7 0.0 copy-start.3
  0.7 0.6 copy-done.4
  1.3 0.0 copy-done.1
  1.3 0.0 copy-done.2
  1.3 0.0 copy-done.3
  1.3 0.6 pad_add_fusion.refs_5_
  1.9 134.2 %shard_map.104 = (f32[8,32,128]{2,1,0:T(8,128)}, f32[8,32,128]{2,1,0:T(8,128)}) custom-call(f32[8,32,128]{2,1,0:T(8,128)} %refs_0_.1, f32[8,32,128]{2,1,0:T(8,128)} %refs_1_.1, f32[8,32,128]{2,1,0:T(8,128)} %refs_2_.1, f32[2,8,32,128]{3,2,1,0:T(8,128)} %refs_3_.1, f32[128,512]{1,0:T(8,128)} %refs_4_.1, s32[4,128]{1,0:T(4,128)} %pad_add_fusion.refs_5_), custom_call_target="tpu_custom_call" | custom-call | tf_op jit(solution)/shard_map/pallas_call | solution.py:566
  136.1 0.0 copy-start
  136.1 1.6 %copy.13 = f32[8,32,128]{2,1,0:T(8,128)} copy(f32[8,32,128]{2,1,0:T(8,128)} %get-tuple-element.4) | data formatting | bytes 262144
  137.7 0.0 copy-done
  137.7 0.7 copy.14
Async XLA Ops:
  0.6 0.7 copy-start.4
  0.6 0.7 copy-start.1
  0.7 0.7 copy-start.2
  0.7 0.7 copy-start.3
  136.1 1.6 %copy-start = (f32[8,32,128]{2,1,0:T(8,128)S(1)}, f32[8,32,128]{2,1,0:T(8,128)}, u32[]{:S(2)}) copy-start(f32[8,32,128]{2,1,0:T(8,128)} %get-tuple-element.5) | copy-start | bytes 393220

commit v4 on v3

--- a/solution.py
+++ b/solution.py
@@ -15,11 +15,11 @@
 MESH = pl.DeviceIdType.MESH
 
 CX0, CY0, H0, W0 = 8, 32, 5, 5
-CX1, CY1, H1, W1 = 4, 16, 3, 3
-CX2, CY2, H2 = 2, 8, 4
+CX1, CY1, H1, HY1 = 4, 16, 10, 16
+CX2, CY2, H2 = 2, 8, 5
 HY = 8
 NX0, NY0 = CX0 + 2 * H0, CY0 + 2 * HY
-NX1, NY1 = CX1 + 2 * H1, CY1 + 2 * HY
+NX1, NY1 = CX1 + 2 * H1, CY1 + 2 * HY1
 NX2, NY2 = CX2 + 2 * H2, CY2 + 2 * HY
 NZ = 128
 
@@ -29,7 +29,7 @@
 
 
 NEAR = ordered([(dx, dy) for dx in (-1, 0, 1) for dy in (-1, 0, 1) if (dx, dy) != (0, 0)])
-WIDE = ordered([(dx, dy) for dx in (-2, -1, 0, 1, 2) for dy in (-1, 0, 1) if (dx, dy) != (0, 0)])
+WIDE = ordered([(dx, dy) for dx in range(-3, 4) for dy in (-1, 0, 1) if (dx, dy) != (0, 0)])
 
 
 def span_x(dx, core, halo, width):
@@ -40,12 +40,12 @@
     return pl.ds(halo, core), pl.ds(halo, core)
 
 
-def span_y(dy, core, width):
+def span_y(dy, core, width, halo=HY):
     if dy > 0:
-        return pl.ds(HY + core - width, width), pl.ds(HY - width, width)
+        return pl.ds(halo + core - width, width), pl.ds(halo - width, width)
     if dy < 0:
-        return pl.ds(HY, width), pl.ds(HY + core, width)
-    return pl.ds(HY, core), pl.ds(HY, core)
+        return pl.ds(halo, width), pl.ds(halo + core, width)
+    return pl.ds(halo, core), pl.ds(halo, core)
 
 
 def strips(ref, core_x, halo, width, core_y):
@@ -63,15 +63,34 @@
     return at
 
 
-def tiles(ref):
+def packed(ref):
+    first, count = H1 // 2, CX1 // 2
+
     def at(dx, dy):
-        sx, tx = pl.ds(H2, CX2), pl.ds(H2 - CX2 * dx, CX2)
-        sy, ty = span_y(dy, CY2, 4)
+        if abs(dx) < 3:
+            sx, tx = pl.ds(first, count), pl.ds(first - count * dx, count)
+        elif dx > 0:
+            sx, tx = pl.ds(first + count - 1, 1), pl.ds(0, 1)
+        else:
+            sx, tx = pl.ds(first, 1), pl.ds(2 * first + count - 1, 1)
+        sy, ty = span_y(dy, CY1, (12, 12, 8, 4)[abs(dx)], HY1)
         if len(ref.shape) == 4:
             return ref.at[:, sx, sy], ref.at[:, tx, ty]
         return ref.at[sx, sy], ref.at[tx, ty]
 
     return at
+
+
+def even_layers(shape):
+    return (lax.broadcasted_iota(jnp.int32, shape, len(shape) - 1) & 1) == 0
+
+
+def unpacked(values):
+    even = even_layers(values.shape)
+    return (
+        jnp.where(even, values, pltpu.roll(values, 1, 1)),
+        jnp.where(even, pltpu.roll(values, NZ - 1, 1), values),
+    )
 
 
 def swap_pair(values, stride):
@@ -149,6 +168,8 @@
     ms0,
     ms1,
     ms2,
+    pks,
+    pk,
     pp,
     xa,
     xb,
@@ -163,7 +184,6 @@
     a1,
     dinv1,
     dg1,
-    r1,
     b2,
     e2a,
     e2b,
@@ -179,12 +199,10 @@
     src_ref,
     s_ms0,
     s_ms1,
-    s_ms2,
     s_pp,
     s_bb,
     s_x,
     s_b1,
-    s_b2,
     s_row,
     s_col,
     s_src,
@@ -248,9 +266,6 @@
     def fine(ref, width):
         return strips(ref, CX0, H0, width, CY0)
 
-    def middle(ref):
-        return strips(ref, CX1, H1, W1, CY1)
-
     def halve(first, second, size, stride):
         pair[pl.ds(0, 2 * size), :] = first + second
         summed = pair[pl.ds(0, size, stride=2), :] + pair[pl.ds(1, size, stride=2), :]
@@ -261,9 +276,10 @@
         pair[pl.ds(1, size, stride=2), :] = values
         return pair[pl.ds(0, 2 * size), :]
 
-    y0, y1, y2 = pl.ds(HY, CY0), pl.ds(HY, CY1), pl.ds(HY, CY2)
-
-    for ref in (ms0, ms1, ms2, pp, xa, xb, bb, b1, e1a, e1b, b2, e2a, e2b, a0, a1, a2, bl, dps, src_ref, dinv0):
+    y0, y1 = pl.ds(HY, CY0), pl.ds(HY1, CY1)
+    even = even_layers((CY1, NZ))
+
+    for ref in (ms0, pk, pks, pp, xa, xb, bb, b1, e1a, e1b, b2, e2a, e2b, a0, a1, a2, bl, dps, src_ref, dinv0):
         ref[...] = jnp.zeros(ref.shape, F32)
     hess_ref[...] = jnp.zeros(hess_ref.shape, F32)
     for i in range(CX0):
@@ -272,12 +288,10 @@
         pp[0, H0 + i, y0] = pert_ref[i]
         pp[1, H0 + i, y0] = press_ref[0, i]
         pp[2, H0 + i, y0] = press_ref[1, i]
-    for i in range(CX1):
-        ms1[0, H1 + i, y1] = halve(log_ref[2 * i], log_ref[2 * i + 1], CY1, 1)
-        ms1[1, H1 + i, y1] = halve(stor_ref[2 * i], stor_ref[2 * i + 1], CY1, 1)
-    for i in range(CX2):
-        for f in range(2):
-            ms2[f, H2 + i, y2] = halve(ms1[f, H1 + 2 * i, y1], ms1[f, H1 + 2 * i + 1, y1], CY2, 2)
+    for f, ref in enumerate((log_ref, stor_ref)):
+        means = [halve(ref[2 * i], ref[2 * i + 1], CY1, 1) for i in range(CX1)]
+        for p in range(CX1 // 2):
+            pks[f, H1 // 2 + p, y1] = jnp.where(even, means[2 * p], means[2 * p + 1])
 
     row_peers = [(lax.rem(gx + k, gx_count), gy) for k in range(1, gx_count)]
     col_peers = [(gx, lax.rem(gy + k, gy_count)) for k in range(1, gy_count)]
@@ -294,14 +308,13 @@
                     barrier, inc=1, device_id=(gx + dx, gy + dy), device_id_type=MESH
                 )
 
-    beside_x = jnp.minimum(gx, 2) + jnp.minimum(gx_count - 1 - gx, 2)
+    beside_x = jnp.minimum(gx, 3) + jnp.minimum(gx_count - 1 - gx, 3)
     beside_y = jnp.minimum(gy, 1) + jnp.minimum(gy_count - 1 - gy, 1)
     pl.semaphore_wait(barrier, beside_x * beside_y + gx_count - 1 + gy_count - 1)
 
     setup = [
         copies(NEAR, s_ms0, fine(ms0, W0)),
-        copies(WIDE, s_ms2, tiles(ms2)),
-        copies(NEAR, s_ms1, middle(ms1)),
+        copies(WIDE, s_ms1, packed(pks)),
         copies(NEAR, s_pp, fine(pp, 3)),
     ]
     for made in setup:
@@ -312,10 +325,16 @@
         copy.start()
     for made in setup:
         finish(made)
+    for f in range(2):
+        for p in range(NX1 // 2):
+            ms1[f, 2 * p], ms1[f, 2 * p + 1] = unpacked(pks[f, p])
+        for j in range(NX2):
+            ms2[f, j] = halve(ms1[f, 2 * j], ms1[f, 2 * j + 1], NY2, 2)
 
     def coefficients(ms, a, dinv, dg, factor, rows, core, halo, core_y, stride):
         ny = ms.shape[2]
-        row = lax.broadcasted_iota(jnp.int32, (ny, NZ), 0) - HY + gy * core_y
+        halo_y = (ny - core_y) // 2
+        row = lax.broadcasted_iota(jnp.int32, (ny, NZ), 0) - halo_y + gy * core_y
         inside_y = jnp.logical_and(row >= 0, row < gy_count * core_y)
         lane = lax.broadcasted_iota(jnp.int32, (ny, NZ), 1)
         for i in rows:
@@ -340,13 +359,9 @@
             scale = jnp.where(jnp.logical_and(inside_y, inside_x), OMEGA / total, 0.0)
             for f in range(6):
                 a[f, i] = faces[f] * scale
-            if core == CX0:
-                dinv[i] = scale
-            elif halo <= i < halo + core:
-                dinv[i - halo] = scale[HY : HY + core_y]
-            if halo <= i < halo + core:
-                if dg is not None:
-                    dg[i - halo] = total[HY : HY + core_y] * (1.0 / OMEGA)
+            dinv[i] = scale
+            if dg is not None:
+                dg[i] = total * (1.0 / OMEGA)
 
     coefficients(ms0, a0, dinv0, dg0, 1.0, range(1, NX0 - 1), CX0, H0, CY0, 1)
     coefficients(ms1, a1, dinv1, dg1, 0.25, range(1, NX1 - 1), CX1, H1, CY1, 2)
@@ -412,14 +427,19 @@
         bb_copies = copies(NEAR, s_bb, fine(bb, W0 - 1))
 
         def cycle(c, inner):
+            turn = s * VCYCLES + c
+            half = lax.rem(turn, 2)
             sweep(xa, xb, bb_right, a0, around(CX0, H0, 2), 1)
             sweep(xb, xa, bb_right, a0, around(CX0, H0, 1), 1)
             for i in range(CX0):
                 old, new = relaxed(xa, bb_right(H0 + i), a0, H0 + i, 1)
-                r0[i] = (new - old)[HY : HY + CY0] * dg0[i]
-            for i in range(CX1):
-                b1[H1 + i, y1] = dinv1[i] * halve(r0[2 * i], r0[2 * i + 1], CY1, 1)
-            made = copies(NEAR, s_b1, middle(b1))
+                r0[i] = ((new - old) * dg0[H0 + i])[HY : HY + CY0]
+            sides = [
+                dinv1[H1 + i, y1] * halve(r0[2 * i], r0[2 * i + 1], CY1, 1) for i in range(CX1)
+            ]
+            for p in range(CX1 // 2):
+                pk[half, H1 // 2 + p, y1] = jnp.where(even, sides[2 * p], sides[2 * p + 1])
+            made = copies(WIDE, s_b1.at[half], packed(pk.at[half]))
             start(made)
 
             @pl.when(c == 0)
@@ -427,33 +447,32 @@
                 start(bb_copies)
 
             finish(made)
-            sweep(b1, e1b, b1_right, a1, around(CX1, H1, 2), 2)
-            for i in range(CX1):
-                old, new = relaxed(e1b, b1[H1 + i], a1, H1 + i, 2)
-                r1[i] = (new - old)[HY : HY + CY1] * dg1[i]
-            for i in range(CX2):
-                b2[H2 + i, y2] = dinv2[i] * halve(r1[2 * i], r1[2 * i + 1], CY2, 2)
-            made = copies(WIDE, s_b2, tiles(b2))
-            start(made)
-            finish(made)
+            for p in range(NX1 // 2):
+                b1[2 * p], b1[2 * p + 1] = unpacked(pk[half, p])
+            sweep(b1, e1b, b1_right, a1, around(CX1, H1, 9), 2)
+            for j in range(1, NX2 - 1):
+                pairs = []
+                for i in (2 * j, 2 * j + 1):
+                    old, new = relaxed(e1b, b1[i], a1, i, 2)
+                    pairs.append((new - old) * dg1[i])
+                b2[j] = dinv2[j] * halve(pairs[0], pairs[1], NY2, 2)
             sweep(b2, e2a, b2_right, a2, around(CX2, H2, 3), 4)
             sweep(e2a, e2b, b2_right, a2, around(CX2, H2, 2), 4)
             sweep(e2b, e2a, b2_right, a2, around(CX2, H2, 1), 4)
             for j in range(CX2 + 2):
-                spread = double(e2a[H2 - 1 + j, pl.ds(HY // 2, CY1)], CY1)
+                spread = double(e2a[H2 - 1 + j], NY2)
                 low = H1 - 2 + 2 * j
                 e1b[low] = e1b[low] + spread
                 e1b[low + 1] = e1b[low + 1] + spread
             sweep(e1b, e1a, b1_right, a1, around(CX1, H1, 1), 2)
             for i in range(CX1):
                 new = relaxed(e1a, b1[H1 + i], a1, H1 + i, 2)[1]
-                spread = double(new[HY : HY + CY1], CY1)
+                spread = double(new[HY1 : HY1 + CY1], CY1)
                 low = H0 + 2 * i
                 xa[low, y0] = xa[low, y0] + spread
                 xa[low + 1, y0] = xa[low + 1, y0] + spread
             made = copies(NEAR, s_x, fine(xa, W0))
             start(made)
-            turn = s * VCYCLES + c
 
             @pl.when(turn == 0)
             def _():
@@ -524,7 +543,7 @@
                 total = jnp.zeros((NY0, NZ), F32)
                 for f in range(6):
                     total = total + a0[f, ext] * (press - presses[f]) * (adjoint - adjoints[f])
-                hess_ref[i] = hess_ref[i] - 0.5 * dg0[i] * total[HY : HY + CY0]
+                hess_ref[i] = hess_ref[i] - (0.5 * dg0[ext] * total)[HY : HY + CY0]
 
         return carry
 
@@ -549,8 +568,6 @@
     ext1 = (NX1, NY1, NZ)
     ext2 = (NX2, NY2, NZ)
     core0 = (CX0, CY0, NZ)
-    core1 = (CX1, CY1, NZ)
-    core2 = (CX2, CY2, NZ)
 
     def vmem(*shape):
         return pltpu.VMEM(shape, F32)
@@ -575,27 +592,28 @@
             vmem(2, *ext0),
             vmem(2, *ext1),
             vmem(2, *ext2),
+            vmem(2, NX1 // 2, NY1, NZ),
+            vmem(2, NX1 // 2, NY1, NZ),
             vmem(3, *ext0),
             vmem(*ext0),
             vmem(*ext0),
             vmem(*ext0),
             vmem(6, *ext0),
             vmem(*ext0),
-            vmem(*core0),
+            vmem(*ext0),
             vmem(*core0),
             vmem(*ext1),
             vmem(*ext1),
             vmem(*ext1),
             vmem(6, *ext1),
-            vmem(*core1),
-            vmem(*core1),
-            vmem(*core1),
+            vmem(*ext1),
+            vmem(*ext1),
             vmem(*ext2),
             vmem(*ext2),
             vmem(*ext2),
             vmem(6, *ext2),
-            vmem(*core2),
-            vmem(CY0, NZ),
+            vmem(*ext2),
+            vmem(NY1, NZ),
             vmem(*ext0),
             vmem(TSTEPS, *ext0),
             vmem(8, NZ),
@@ -604,13 +622,11 @@
             vmem(gy_count - 1, 8, NZ),
             vmem(TSTEPS, *ext0),
             sems(len(NEAR)),
-            sems(len(NEAR)),
             sems(len(WIDE)),
             sems(len(NEAR)),
             sems(len(NEAR)),
             sems(len(NEAR)),
-            sems(len(NEAR)),
-            sems(len(WIDE)),
+            pltpu.SemaphoreType.DMA((2, 2, len(WIDE))),
             sems(gx_count - 1),
             sems(gy_count - 1),
             sems(len(NEAR)),

time: 139 us -> 124 us (0.89)
  Pallas kernels: 134 us -> 120 us
    pallas_call x1, Pallas kernels: 134 us -> 120 us  [local(): pl.pallas_call(body, out_shape=(jax.ShapeDtypeStruct(core0, F32), jax.Sha...]
where the time goes in v4:
time: 124 us
  Pallas kernels  120 us (97%)
  local copies, waits for them, and re-layouts  2.93 us (2%)
    pallas_call x1, Pallas kernels, local(): pl.pallas_call(body, out_shape=(jax.ShapeDtypeStruct(core0, F32), jax.Sha...  120 us
    unnamed x12, local copies, waits for them, and re-layouts  2.93 us

profile of v4, /device:TPU:3, one launch (start us, length us, event | category | flops | bytes accessed | tf_op | source)
XLA Modules:
  0.0 123.7 jit_solution(14328831961949175017)
XLA Ops:
  0.6 0.0 copy-start.4
  0.6 0.0 copy-start.1
  0.7 0.0 copy-start.2
  0.7 0.0 copy-start.3
  0.7 0.6 copy-done.4
  1.3 0.0 copy-done.1
  1.3 0.0 copy-done.2
  1.3 0.0 copy-done.3
  1.3 0.6 pad_add_fusion.refs_5_
  1.9 119.5 %shard_map.104 = (f32[8,32,128]{2,1,0:T(8,128)}, f32[8,32,128]{2,1,0:T(8,128)}) custom-call(f32[8,32,128]{2,1,0:T(8,128)} %refs_0_.1, f32[8,32,128]{2,1,0:T(8,128)} %refs_1_.1, f32[8,32,128]{2,1,0:T(8,128)} %refs_2_.1, f32[2,8,32,128]{3,2,1,0:T(8,128)} %refs_3_.1, f32[128,512]{1,0:T(8,128)} %refs_4_.1, s32[4,128]{1,0:T(4,128)} %pad_add_fusion.refs_5_), custom_call_target="tpu_custom_call" | custom-call | tf_op jit(solution)/shard_map/pallas_call | solution.py:583
  121.5 0.0 copy-start
  121.5 1.6 %copy.13 = f32[8,32,128]{2,1,0:T(8,128)} copy(f32[8,32,128]{2,1,0:T(8,128)} %get-tuple-element.4) | data formatting | bytes 262144
  123.1 0.0 copy-done
  123.1 0.7 copy.14
Async XLA Ops:
  0.6 0.7 copy-start.4
  0.6 0.7 copy-start.1
  0.7 0.7 copy-start.2
  0.7 0.7 copy-start.3
  121.5 1.6 %copy-start = (f32[8,32,128]{2,1,0:T(8,128)S(1)}, f32[8,32,128]{2,1,0:T(8,128)}, u32[]{:S(2)}) copy-start(f32[8,32,128]{2,1,0:T(8,128)} %get-tuple-element.5) | copy-start | bytes 393220

commit v5 on v4

--- a/solution.py
+++ b/solution.py
@@ -323,14 +323,6 @@
     row_copies = spread(listed, by_row, s_row, row_peers)
     for copy in row_copies:
         copy.start()
-    for made in setup:
-        finish(made)
-    for f in range(2):
-        for p in range(NX1 // 2):
-            ms1[f, 2 * p], ms1[f, 2 * p + 1] = unpacked(pks[f, p])
-        for j in range(NX2):
-            ms2[f, j] = halve(ms1[f, 2 * j], ms1[f, 2 * j + 1], NY2, 2)
-
     def coefficients(ms, a, dinv, dg, factor, rows, core, halo, core_y, stride):
         ny = ms.shape[2]
         halo_y = (ny - core_y) // 2
@@ -363,9 +355,17 @@
             if dg is not None:
                 dg[i] = total * (1.0 / OMEGA)
 
+    finish(setup[0])
     coefficients(ms0, a0, dinv0, dg0, 1.0, range(1, NX0 - 1), CX0, H0, CY0, 1)
+    finish(setup[1])
+    for f in range(2):
+        for p in range(NX1 // 2):
+            ms1[f, 2 * p], ms1[f, 2 * p + 1] = unpacked(pks[f, p])
+        for j in range(NX2):
+            ms2[f, j] = halve(ms1[f, 2 * j], ms1[f, 2 * j + 1], NY2, 2)
     coefficients(ms1, a1, dinv1, dg1, 0.25, range(1, NX1 - 1), CX1, H1, CY1, 2)
     coefficients(ms2, a2, dinv2, None, 0.0625, range(1, NX2 - 1), CX2, H2, CY2, 4)
+    finish(setup[2])
 
     def relaxed(src, right, a, i, stride):
         ny = src.shape[0 if src.ndim == 2 else 1]
@@ -429,7 +429,15 @@
         def cycle(c, inner):
             turn = s * VCYCLES + c
             half = lax.rem(turn, 2)
-            sweep(xa, xb, bb_right, a0, around(CX0, H0, 2), 1)
+            @pl.when(c == 0)
+            def _():
+                for i in around(CX0, H0, 2):
+                    xb[i] = bl[i]
+
+            @pl.when(c > 0)
+            def _():
+                sweep(xa, xb, bb_right, a0, around(CX0, H0, 2), 1)
+
             sweep(xb, xa, bb_right, a0, around(CX0, H0, 1), 1)
             for i in range(CX0):
                 old, new = relaxed(xa, bb_right(H0 + i), a0, H0 + i, 1)

time: 124 us -> 122 us (0.984)
  Pallas kernels: 120 us -> 117 us
    pallas_call x1, Pallas kernels: 120 us -> 117 us  [local(): pl.pallas_call(body, out_shape=(jax.ShapeDtypeStruct(core0, F32), jax.Sha...]
where the time goes in v5:
time: 122 us
  Pallas kernels  117 us (96%)
  local copies, waits for them, and re-layouts  2.93 us (2%)
    pallas_call x1, Pallas kernels, local(): pl.pallas_call(body, out_shape=(jax.ShapeDtypeStruct(core0, F32), jax.Sha...  117 us
    unnamed x12, local copies, waits for them, and re-layouts  2.93 us

profile of v5, /device:TPU:3, one launch (start us, length us, event | category | flops | bytes accessed | tf_op | source)
XLA Modules:
  0.0 121.5 jit_solution(7815297728739368048)
XLA Ops:
  0.6 0.0 copy-start.4
  0.6 0.0 copy-start.1
  0.7 0.0 copy-start.2
  0.7 0.0 copy-start.3
  0.7 0.6 copy-done.4
  1.3 0.0 copy-done.1
  1.3 0.0 copy-done.2
  1.3 0.0 copy-done.3
  1.3 0.6 pad_add_fusion.refs_5_
  1.9 117.3 %shard_map.104 = (f32[8,32,128]{2,1,0:T(8,128)}, f32[8,32,128]{2,1,0:T(8,128)}) custom-call(f32[8,32,128]{2,1,0:T(8,128)} %refs_0_.1, f32[8,32,128]{2,1,0:T(8,128)} %refs_1_.1, f32[8,32,128]{2,1,0:T(8,128)} %refs_2_.1, f32[2,8,32,128]{3,2,1,0:T(8,128)} %refs_3_.1, f32[128,512]{1,0:T(8,128)} %refs_4_.1, s32[4,128]{1,0:T(4,128)} %pad_add_fusion.refs_5_), custom_call_target="tpu_custom_call" | custom-call | tf_op jit(solution)/shard_map/pallas_call | solution.py:591
  119.2 0.0 copy-start
  119.3 1.6 %copy.13 = f32[8,32,128]{2,1,0:T(8,128)} copy(f32[8,32,128]{2,1,0:T(8,128)} %get-tuple-element.4) | data formatting | bytes 262144
  120.9 0.0 copy-done
  120.9 0.7 copy.14
Async XLA Ops:
  0.6 0.7 copy-start.4
  0.6 0.7 copy-start.1
  0.7 0.7 copy-start.2
  0.7 0.7 copy-start.3
  119.2 1.6 %copy-start = (f32[8,32,128]{2,1,0:T(8,128)S(1)}, f32[8,32,128]{2,1,0:T(8,128)}, u32[]{:S(2)}) copy-start(f32[8,32,128]{2,1,0:T(8,128)} %get-tuple-element.5) | copy-start | bytes 393220

commit v6 on v5

--- a/solution.py
+++ b/solution.py
@@ -279,9 +279,8 @@
     y0, y1 = pl.ds(HY, CY0), pl.ds(HY1, CY1)
     even = even_layers((CY1, NZ))
 
-    for ref in (ms0, pk, pks, pp, xa, xb, bb, b1, e1a, e1b, b2, e2a, e2b, a0, a1, a2, bl, dps, src_ref, dinv0):
+    for ref in (ms0, pk, pks, pp, bb):
         ref[...] = jnp.zeros(ref.shape, F32)
-    hess_ref[...] = jnp.zeros(hess_ref.shape, F32)
     for i in range(CX0):
         ms0[0, H0 + i, y0] = log_ref[i]
         ms0[1, H0 + i, y0] = stor_ref[i]
@@ -319,6 +318,8 @@
     ]
     for made in setup:
         start(made)
+    for ref in (xa, src_ref, hess_ref):
+        ref[...] = jnp.zeros(ref.shape, F32)
     list_wells(rows_ref, ints_ref, listed)
     row_copies = spread(listed, by_row, s_row, row_peers)
     for copy in row_copies:

time: 122 us -> 120 us (0.984)
    pallas_call x1, Pallas kernels: 117 us -> 116 us  [local(): pl.pallas_call(body, out_shape=(jax.ShapeDtypeStruct(core0, F32), jax.Sha...]
where the time goes in v6:
time: 120 us
  Pallas kernels  116 us (97%)
  local copies, waits for them, and re-layouts  2.93 us (2%)
    pallas_call x1, Pallas kernels, local(): pl.pallas_call(body, out_shape=(jax.ShapeDtypeStruct(core0, F32), jax.Sha...  116 us
    unnamed x12, local copies, waits for them, and re-layouts  2.93 us

profile of v6, /device:TPU:3, one launch (start us, length us, event | category | flops | bytes accessed | tf_op | source)
XLA Modules:
  0.0 120.1 jit_solution(1515235470732693273)
XLA Ops:
  0.6 0.0 copy-start.4
  0.6 0.0 copy-start.1
  0.7 0.0 copy-start.2
  0.7 0.0 copy-start.3
  0.7 0.6 copy-done.4
  1.3 0.0 copy-done.1
  1.3 0.0 copy-done.2
  1.3 0.0 copy-done.3
  1.3 0.6 pad_add_fusion.refs_5_
  1.9 115.9 %shard_map.104 = (f32[8,32,128]{2,1,0:T(8,128)}, f32[8,32,128]{2,1,0:T(8,128)}) custom-call(f32[8,32,128]{2,1,0:T(8,128)} %refs_0_.1, f32[8,32,128]{2,1,0:T(8,128)} %refs_1_.1, f32[8,32,128]{2,1,0:T(8,128)} %refs_2_.1, f32[2,8,32,128]{3,2,1,0:T(8,128)} %refs_3_.1, f32[128,512]{1,0:T(8,128)} %refs_4_.1, s32[4,128]{1,0:T(4,128)} %pad_add_fusion.refs_5_), custom_call_target="tpu_custom_call" | custom-call | tf_op jit(solution)/shard_map/pallas_call | solution.py:592
  117.9 0.0 copy-start
  117.9 1.6 %copy.13 = f32[8,32,128]{2,1,0:T(8,128)} copy(f32[8,32,128]{2,1,0:T(8,128)} %get-tuple-element.4) | data formatting | bytes 262144
  119.5 0.0 copy-done
  119.5 0.7 copy.14
Async XLA Ops:
  0.6 0.7 copy-start.4
  0.6 0.7 copy-start.1
  0.7 0.7 copy-start.2
  0.7 0.7 copy-start.3
  117.9 1.6 %copy-start = (f32[8,32,128]{2,1,0:T(8,128)S(1)}, f32[8,32,128]{2,1,0:T(8,128)}, u32[]{:S(2)}) copy-start(f32[8,32,128]{2,1,0:T(8,128)} %get-tuple-element.5) | copy-start | bytes 393220

commit v7 on v6

--- a/solution.py
+++ b/solution.py
@@ -450,12 +450,12 @@
                 pk[half, H1 // 2 + p, y1] = jnp.where(even, sides[2 * p], sides[2 * p + 1])
             made = copies(WIDE, s_b1.at[half], packed(pk.at[half]))
             start(made)
+            finish(made)
 
             @pl.when(c == 0)
             def _():
                 start(bb_copies)
 
-            finish(made)
             for p in range(NX1 // 2):
                 b1[2 * p], b1[2 * p + 1] = unpacked(pk[half, p])
             sweep(b1, e1b, b1_right, a1, around(CX1, H1, 9), 2)

time: 120 us -> 121 us (level)
  no operation moved by 1% of the time
where the time goes in v7:
time: 121 us; the launch traced here: 120 us
  Pallas kernels  116 us (96%)
  local copies, waits for them, and re-layouts  2.93 us (2%)
    pallas_call x1, Pallas kernels, local(): pl.pallas_call(body, out_shape=(jax.ShapeDtypeStruct(core0, F32), jax.Sha...  116 us
    unnamed x12, local copies, waits for them, and re-layouts  2.93 us

profile of v7, /device:TPU:3, one launch (start us, length us, event | category | flops | bytes accessed | tf_op | source)
XLA Modules:
  0.0 120.5 jit_solution(194009883280299152)
XLA Ops:
  0.6 0.0 copy-start.4
  0.6 0.0 copy-start.1
  0.7 0.0 copy-start.2
  0.7 0.0 copy-start.3
  0.7 0.6 copy-done.4
  1.3 0.0 copy-done.1
  1.3 0.0 copy-done.2
  1.3 0.0 copy-done.3
  1.3 0.6 pad_add_fusion.refs_5_
  1.9 116.3 %shard_map.104 = (f32[8,32,128]{2,1,0:T(8,128)}, f32[8,32,128]{2,1,0:T(8,128)}) custom-call(f32[8,32,128]{2,1,0:T(8,128)} %refs_0_.1, f32[8,32,128]{2,1,0:T(8,128)} %refs_1_.1, f32[8,32,128]{2,1,0:T(8,128)} %refs_2_.1, f32[2,8,32,128]{3,2,1,0:T(8,128)} %refs_3_.1, f32[128,512]{1,0:T(8,128)} %refs_4_.1, s32[4,128]{1,0:T(4,128)} %pad_add_fusion.refs_5_), custom_call_target="tpu_custom_call" | custom-call | tf_op jit(solution)/shard_map/pallas_call | solution.py:592
  118.2 0.0 copy-start
  118.2 1.6 %copy.13 = f32[8,32,128]{2,1,0:T(8,128)} copy(f32[8,32,128]{2,1,0:T(8,128)} %get-tuple-element.4) | data formatting | bytes 262144
  119.8 0.0 copy-done
  119.8 0.7 copy.14
Async XLA Ops:
  0.6 0.7 copy-start.4
  0.6 0.7 copy-start.1
  0.7 0.7 copy-start.2
  0.7 0.7 copy-start.3
  118.2 1.6 %copy-start = (f32[8,32,128]{2,1,0:T(8,128)S(1)}, f32[8,32,128]{2,1,0:T(8,128)}, u32[]{:S(2)}) copy-start(f32[8,32,128]{2,1,0:T(8,128)} %get-tuple-element.5) | copy-start | bytes 393220
